TPU v7x, 256 devices: a whole 4x4x8 slice. The times are simulated.
256 devices in a mesh: seq: 4 (over x_lo, core), dp: 64 (over x_hi, y, z).
Axes of the slice: x: 4 (x_hi: 2, x_lo: 2; x = x_hi * 2 + x_lo), y: 4, z: 8, core: 2. Of those that a mesh axis runs over, the one named last changes fastest.
Arguments:
- residual: bfloat16 [49152, 2560], P(('seq', 'dp')), may hold values from -6 to 6
- query_raw: bfloat16 [49152, 2560], P(('seq', 'dp')), may hold values from -60 to 60
- key_raw: bfloat16 [49152, 2560], P(('seq', 'dp')), may hold values from -60 to 60
- values: bfloat16 [49152, 2560], P(('seq', 'dp')), may hold values from -6 to 6
- residual_grad: bfloat16 [49152, 2560], P(('seq', 'dp')), may hold values from -6 to 6
- modulated_grad: bfloat16 [49152, 2560], P(('seq', 'dp')), may hold values from -24 to 24
- condition: float32 [64, 2, 2560], P('dp'), may hold values from -3 to 3
- modulation: float32 [2, 2560], P(None, ('seq', 'dp')), may hold values from -0.5 to 0.5
- norm_gains: float32 [2, 2560], P(None, ('seq', 'dp')), may hold values from 0.25 to 1.75
Outputs:
- input_grad: bfloat16 [49152, 2560], P(('seq', 'dp'))
- query_grad: bfloat16 [49152, 2560], P(('seq', 'dp'))
- key_grad: bfloat16 [49152, 2560], P(('seq', 'dp'))
- value_grad: bfloat16 [49152, 2560], P(('seq', 'dp'))
- param_grads: float32 [5, 2560], P(None, ('seq', 'dp'))
All inputs are finite; a program needn't handle non-finite values.
Results may differ from a plain program's by a relative error of at most 0.009.
The roundings to bfloat16 on the way count: a program that leaves them out, or rounds other values in their place, can miss the bound.
Values may be sent and summed in bfloat16 or wider, within the bound.
A program may use at most 128 MiB of HBM per device.

v0:
```python
import jax
import jax.numpy as jnp
from jax import lax
from jax.sharding import PartitionSpec as P

HEAD_DIM = 128


epsilon = 1e-06


def root_scale(raw_values):
    floats = raw_values.astype(jnp.float32)
    return lax.rsqrt(jnp.mean(floats * floats, axis=1, keepdims=True) + epsilon)


def head_scores(query_head, key_head):
    return lax.dot_general(
        query_head, key_head, (((1,), (1,)), ((), ())), preferred_element_type=jnp.float32
    ) * query_head.shape[-1] ** (-0.5)


def head_forward(pieces):
    query_head, key_head, value_head = pieces
    scores = head_scores(query_head, key_head)
    row_max = jnp.max(scores, axis=1, keepdims=True)
    row_sum = jnp.sum(jnp.exp(scores - row_max), axis=1, keepdims=True)
    logsum = row_max + jnp.log(row_sum)
    weights_low = jnp.exp(scores - logsum).astype(jnp.bfloat16)
    attended = jnp.dot(weights_low, value_head, preferred_element_type=jnp.float32).astype(
        jnp.bfloat16
    )
    return (attended, logsum[:, 0])


def head_backward(pieces):
    query_head, key_head, value_head, attended, attended_grad, logsum = pieces
    scores = head_scores(query_head, key_head)
    weights = jnp.exp(scores - logsum[:, None])
    row_dot = jnp.sum(
        attended_grad.astype(jnp.float32) * attended.astype(jnp.float32), axis=1, keepdims=True
    )
    weight_grad = lax.dot_general(
        attended_grad, value_head, (((1,), (1,)), ((), ())), preferred_element_type=jnp.float32
    )
    score_grad = (weights * (weight_grad - row_dot) * query_head.shape[-1] ** (-0.5)).astype(
        jnp.bfloat16
    )
    value_part = lax.dot_general(
        weights.astype(jnp.bfloat16),
        attended_grad,
        (((0,), (0,)), ((), ())),
        preferred_element_type=jnp.float32,
    )
    query_part = jnp.dot(score_grad, key_head, preferred_element_type=jnp.float32)
    key_part = lax.dot_general(
        score_grad, query_head, (((0,), (0,)), ((), ())), preferred_element_type=jnp.float32
    )
    return (query_part, key_part, value_part)


def stream_pass(residual, attended, modulated, residual_grad, modulated_grad):
    gate_row = modulated[0]
    scale_row = modulated[1]
    summed = residual.astype(jnp.float32) + gate_row * attended.astype(jnp.float32)
    centered = summed - jnp.mean(summed, axis=1, keepdims=True)
    norm_scale = lax.rsqrt(jnp.mean(centered * centered, axis=1, keepdims=True) + epsilon)
    normed = centered * norm_scale
    scaled_grad = modulated_grad.astype(jnp.float32) * (1.0 + scale_row)
    stream_grad = residual_grad.astype(jnp.float32) + norm_scale * (
        scaled_grad
        - jnp.mean(scaled_grad, axis=1, keepdims=True)
        - normed * jnp.mean(scaled_grad * normed, axis=1, keepdims=True)
    )
    attended_grad = (stream_grad * gate_row).astype(jnp.bfloat16)
    return (stream_grad, normed, attended_grad)


def norm_backward(raw_values, inverse, gain_row, upstream):
    floats = raw_values.astype(jnp.float32)
    weighted = gain_row * upstream
    return (
        inverse * weighted
        - floats * inverse**3 * jnp.mean(floats * weighted, axis=1, keepdims=True)
    ).astype(jnp.bfloat16)


def partial_sums(
    attended,
    stream_grad,
    normed,
    modulated_grad,
    query_raw,
    query_scale,
    query_part,
    key_raw,
    key_scale,
    key_part,
):
    grad_floats = modulated_grad.astype(jnp.float32)
    return jnp.stack(
        [
            jnp.sum(stream_grad * attended.astype(jnp.float32), axis=0),
            jnp.sum(grad_floats, axis=0),
            jnp.sum(grad_floats * normed, axis=0),
            jnp.sum(query_part * query_raw.astype(jnp.float32) * query_scale, axis=0),
            jnp.sum(key_part * key_raw.astype(jnp.float32) * key_scale, axis=0),
        ]
    )


def per_device(
    residual,
    query_raw,
    key_raw,
    values,
    residual_grad,
    modulated_grad,
    condition,
    modulation,
    norm_gains,
):
    head_width = HEAD_DIM
    row_count = residual.shape[0]
    modulation_all, gains_all = (
        lax.all_gather(modulation, ("seq", "dp"), axis=1, tiled=True),
        lax.all_gather(norm_gains, ("seq", "dp"), axis=1, tiled=True),
    )
    modulated = modulation_all + condition[0]
    query_scale = root_scale(query_raw)
    key_scale = root_scale(key_raw)
    normed_query = (query_raw.astype(jnp.float32) * query_scale * gains_all[0]).astype(jnp.bfloat16)
    normed_key = (key_raw.astype(jnp.float32) * key_scale * gains_all[1]).astype(jnp.bfloat16)
    query_moved, key_moved, value_moved = (
        lax.all_to_all(
            normed_query.reshape(row_count, -1, head_width),
            "seq",
            split_axis=1,
            concat_axis=0,
            tiled=True,
        ),
        lax.all_to_all(
            normed_key.reshape(row_count, -1, head_width),
            "seq",
            split_axis=1,
            concat_axis=0,
            tiled=True,
        ),
        lax.all_to_all(
            values.reshape(row_count, -1, head_width),
            "seq",
            split_axis=1,
            concat_axis=0,
            tiled=True,
        ),
    )
    query_heads = query_moved.transpose(1, 0, 2)
    key_heads = key_moved.transpose(1, 0, 2)
    value_heads = value_moved.transpose(1, 0, 2)
    attended_heads, logsum = lax.map(head_forward, (query_heads, key_heads, value_heads))
    attended_tokens = lax.all_to_all(
        attended_heads.transpose(1, 0, 2), "seq", split_axis=0, concat_axis=1, tiled=True
    )
    attended = attended_tokens.reshape(row_count, -1)
    stream_grad, normed, attended_grad = stream_pass(
        residual, attended, modulated, residual_grad, modulated_grad
    )
    grad_moved = lax.all_to_all(
        attended_grad.reshape(row_count, -1, head_width),
        "seq",
        split_axis=1,
        concat_axis=0,
        tiled=True,
    )
    query_part, key_part, value_part = lax.map(
        head_backward,
        (
            query_heads,
            key_heads,
            value_heads,
            attended_heads,
            grad_moved.transpose(1, 0, 2),
            logsum,
        ),
    )
    query_back, key_back, value_back = (
        lax.all_to_all(
            query_part.transpose(1, 0, 2), "seq", split_axis=0, concat_axis=1, tiled=True
        ),
        lax.all_to_all(key_part.transpose(1, 0, 2), "seq", split_axis=0, concat_axis=1, tiled=True),
        lax.all_to_all(
            value_part.transpose(1, 0, 2), "seq", split_axis=0, concat_axis=1, tiled=True
        ),
    )
    query_grad_n = query_back.reshape(row_count, -1)
    key_grad_n = key_back.reshape(row_count, -1)
    value_sum = value_back.reshape(row_count, -1)
    sums_here = partial_sums(
        attended,
        stream_grad,
        normed,
        modulated_grad,
        query_raw,
        query_scale,
        query_grad_n,
        key_raw,
        key_scale,
        key_grad_n,
    )
    reduced = lax.psum_scatter(sums_here, ("seq", "dp"), scatter_dimension=1, tiled=True)
    factor = (row_count * lax.axis_size("seq") * lax.axis_size("dp")) ** (-0.5)
    return (
        stream_grad.astype(jnp.bfloat16),
        norm_backward(query_raw, query_scale, gains_all[0], query_grad_n),
        norm_backward(key_raw, key_scale, gains_all[1], key_grad_n),
        value_sum.astype(jnp.bfloat16),
        reduced * factor,
    )


def solution(mesh):
    placed = (
        P(("seq", "dp"), None),
        P(("seq", "dp"), None),
        P(("seq", "dp"), None),
        P(("seq", "dp"), None),
        P(("seq", "dp"), None),
        P(("seq", "dp"), None),
        P("dp", None, None),
        P(None, ("seq", "dp")),
        P(None, ("seq", "dp")),
    )
    return jax.shard_map(
        per_device,
        mesh=mesh,
        in_specs=placed,
        out_specs=(
            P(("seq", "dp"), None),
            P(("seq", "dp"), None),
            P(("seq", "dp"), None),
            P(("seq", "dp"), None),
            P(None, ("seq", "dp")),
        ),
        check_vma=False,
    )
```

profile of v0, /device:TPU:1, one launch (start us, length us, event | category | flops | bytes accessed | tf_op | source)
XLA Modules:
  0.0 1958.0 jit_solution(11873094181766818667)
XLA Ops:
  3.0 6.7 all-to-all-start.2
  9.8 647.2 %all-gather.1 = f32[256,10,2]{1,2,0:T(2,128)S(1)} all-gather(f32[1,10,2]{1,2,0:T(2,128)S(1)} %bitcast.194), channel_id=1, replica_groups=mesh['seq'=4,'dp'=64] {'seq','dp'}, dimensions={0}, use_global_device_ids=true | all-gather | bytes 20560 | tf_op jit(solution)/shard_map/all_gather | solution.py:127
  658.8 2.4 copy.77
  663.5 3.5 fusion.55
  667.0 2.4 copy.79
  669.4 4.2 all-to-all-start.1
  673.5 2.4 copy.75
  675.9 10.5 all-to-all-done.1
  686.4 5.1 all-to-all-start
  691.5 664.9 %all-gather = f32[256,10,2]{1,2,0:T(2,128)S(1)} all-gather(f32[1,10,2]{1,2,0:T(2,128)S(1)} %bitcast.195), channel_id=1, replica_groups=mesh['seq'=4,'dp'=64] {'seq','dp'}, dimensions={0}, use_global_device_ids=true | all-gather | bytes 20560 | tf_op jit(solution)/shard_map/all_gather | solution.py:126
  1357.2 2.4 copy.85
  1359.6 2.4 copy.70
  1361.9 2.4 copy.69
  1368.5 27.5 %while.26 = (s32[]{:T(128)}, bf16[5,768,128]{2,1,0:T(8,128)(2,1)}, f32[5,768]{1,0:T(8,128)}, bf16[5,768,128]{2,1,0:T(8,128)(2,1)}, bf16[5,768,128]{2,1,0:T(8,128...) while((s32[]{:T(128)}, bf16[5,768,128]{2,1,0:T(8,128)(2,1)}, f32[5,768]{1,0:T(8,128)}, ...), condition=%wide.region_5.6_spmd, body=%wide.region_2.5_spmd.sunk | while | flops 306806016 | bytes 7900257 | solution.py:160
  1396.0 3.1 copy.129
  1399.1 4.7 all-to-all-start.3
  1403.9 19.2 all-to-all-done.3
  1423.1 3.1 copy.84
  1426.3 2.6 fusion.75
  1436.3 2.4 copy.87
  1438.7 4.3 all-to-all-start.4
  1443.0 12.9 all-to-all-done.4
  1457.1 218.5 %while.27 = (s32[]{:T(128)}, f32[5,768,128]{2,0,1:T(8,128)}, f32[5,768,128]{2,0,1:T(8,128)}, bf16[5,768,128]{2,0,1:T(8,128)(2,1)}, bf16[5,768,128]{2,1,0:T(8,128...) while((s32[]{:T(128)}, f32[5,768,128]{2,0,1:T(8,128)}, ...), condition=%wide.region_12.13_spmd, body=%wide.region_10.12_spmd.sunk | while | flops 760675584 | bytes 15945885 | solution.py:175
  1466.9 11.0 dynamic_update_slice.28
  1477.9 11.4 dynamic_update_slice.27
  1489.3 11.4 dynamic_update_slice.26
  1510.6 11.0 dynamic_update_slice.28
  1521.6 11.4 dynamic_update_slice.27
  1533.0 11.4 dynamic_update_slice.26
  1554.3 11.0 dynamic_update_slice.28
  1565.3 11.4 dynamic_update_slice.27
  1576.7 11.4 dynamic_update_slice.26
  1598.0 11.0 dynamic_update_slice.28
  1609.0 11.4 dynamic_update_slice.27
  1620.4 11.4 dynamic_update_slice.26
  1641.7 11.0 dynamic_update_slice.28
  1652.7 11.4 dynamic_update_slice.27
  1664.1 11.4 dynamic_update_slice.26
  1675.5 24.6 %all_to_all.120 = bf16[768,5,128]{2,1,0:T(8,128)(2,1)} all-to-all(bf16[768,5,128]{2,1,0:T(8,128)(2,1)} %bitcast.192), channel_id=1, replica_groups=mesh['seq'=4,'dp'=64] {'seq'}, dimensions={0} | all-to-all | bytes 1966080 | tf_op jit(solution)/shard_map/all_to_all | solution.py:191
  1700.1 40.3 %all_to_all.121 = f32[768,5,128]{2,1,0:T(8,128)} all-to-all(f32[768,5,128]{2,1,0:T(8,128)S(1)} %bitcast.191), channel_id=1, replica_groups=mesh['seq'=4,'dp'=64] {'seq'}, dimensions={0} | all-to-all | bytes 3932160 | tf_op jit(solution)/shard_map/all_to_all | solution.py:187
  1740.4 5.6 all-to-all-start.6
  1748.4 2.6 copy.94
  1753.3 3.3 copy.90
  1756.7 25.5 %all-to-all-done.6 = f32[768,5,128]{2,1,0:T(8,128)} async-done(((f32[768,5,128]{2,1,0:T(8,128)}), f32[768,5,128]{2,1,0:T(8,128)}, u32[]{:S(2)}, u32[]{:S(2)}) %all-to-all-start.6) | async-done | bytes 1966112 | tf_op jit(solution)/shard_map/all_to_all | solution.py:190
  1782.2 3.4 copy.92
  1785.6 3.3 fusion.70
  1793.0 2.9 fusion.61
  1800.0 157.2 %all-reduce = f32[5,2560]{1,0:T(8,128)S(1)} all-reduce(f32[5,2560]{1,0:T(8,128)S(1)} %stack.23), channel_id=2, replica_groups=mesh['seq'=4,'dp'=64] {'seq','dp'}, use_global_device_ids=true, to_apply=%region_20.21.clone | all-reduce | flops 12800 | bytes 102400
  (152 shorter events, 110.2 us)
Async XLA Ops:
  0.6 1.2 copy-start
  0.6 9.1 copy-start.18
  0.7 656.6 %copy-start.9 = (bf16[192,2560]{1,0:T(8,128)(2,1)S(1)}, bf16[192,2560]{1,0:T(8,128)(2,1)}, u32[]{:S(2)}) copy-start(bf16[192,2560]{1,0:T(8,128)(2,1)} %param.14) | copy-start | bytes 2949124
  3.0 666.3 %all-to-all-start.2 = ((bf16[192,20,128]{2,0,1:T(8,128)(2,1)}), bf16[192,20,128]{2,0,1:T(8,128)(2,1)S(1)}, u32[]{:S(2)}, u32[]{:S(2)}) async-start(bf16[192,20,128]{2,0,1:T(8,128)(2,1)} %copy_bitcast_fusion.1), calls=%async_computation.2 | async-start | bytes 1966080 | tf_op jit(solution)/shard_map/all_to_all | solution.py:149
  657.2 6.3 copy-start.10
  663.5 3.5 copy-start.14
  669.4 17.1 all-to-all-start.1
  673.5 18.0 copy-start.19
  686.4 679.9 %all-to-all-start = ((bf16[192,20,128]{2,0,1:T(8,128)(2,1)}), bf16[192,20,128]{2,0,1:T(8,128)(2,1)}, u32[]{:S(2)}, u32[]{:S(2)}) async-start(bf16[192,20,128]{2,0,1:T(8,128)(2,1)} %copy.75), calls=%async_computation | async-start | bytes 1966080 | tf_op jit(solution)/shard_map/all_to_all | solution.py:135
  1396.0 7.8 copy-start.12
  1396.0 7.8 copy-start.13
  1399.1 24.0 %all-to-all-start.3 = ((bf16[768,5,128]{2,1,0:T(8,128)(2,1)}), bf16[768,5,128]{2,1,0:T(8,128)(2,1)}, u32[]{:S(2)}, u32[]{:S(2)}) async-start(bf16[768,5,128]{2,1,0:T(8,128)(2,1)} %bitcast.181), calls=%async_computation.3 | async-start | bytes 3145728 | tf_op jit(solution)/shard_map/all_to_all | solution.py:161
  1428.8 1.3 copy-start.6
  1429.2 3.0 copy-start.5
  1429.2 3.0 copy-start.7
  1438.7 17.2 all-to-all-start.4
  1675.5 24.6 %copy-start.8 = (f32[5,768,128]{2,0,1:T(8,128)S(1)}, f32[5,768,128]{2,0,1:T(8,128)}, u32[]{:S(2)}) copy-start(f32[5,768,128]{2,0,1:T(8,128)} %get-tuple-element.94) | copy-start | bytes 5898244
  1740.4 41.8 %all-to-all-start.6 = ((f32[768,5,128]{2,1,0:T(8,128)}), f32[768,5,128]{2,1,0:T(8,128)}, u32[]{:S(2)}, u32[]{:S(2)}) async-start(f32[768,5,128]{2,1,0:T(8,128)} %bitcast.190), calls=%async_computation.6 | async-start | bytes 6291456 | tf_op jit(solution)/shard_map/all_to_all | solution.py:190
  1782.2 3.4 copy-start.11
  1782.2 3.4 copy-start.15
  1785.6 3.4 copy-start.2
  1785.6 3.4 copy-start.4
  1785.6 3.4 copy-start.17
  1790.6 5.3 copy-start.16
  1793.0 3.0 copy-start.3
  1795.9 162.0 %copy-start.1 = (bf16[192,2560]{1,0:T(8,128)(2,1)S(1)}, bf16[192,2560]{1,0:T(8,128)(2,1)}, u32[]{:S(2)}) copy-start(bf16[192,2560]{1,0:T(8,128)(2,1)} %param.16) | copy-start | bytes 2949124
where the time goes:
time: 1960 us
  blocking collectives  1530 us (78%)
  local copies, waits for them, and re-layouts  232 us (12%)
  waiting for transfers between devices  68.1 us (3%)
  matrix products  57.8 us (3%)
  other arithmetic  34.3 us (2%)
  starting transfers between devices  30.7 us (2%)
    all_gather x1, blocking collectives, per_device(): lax.all_gather(modulation, ('seq', 'dp'), axis=1, tiled=True)  665 us
    all_gather x1, blocking collectives, per_device(): lax.all_gather(norm_gains, ('seq', 'dp'), axis=1, tiled=True)  647 us
    dynamic_update_slice x15, local copies, waits for them, and re-layouts, per_device(): lax.map(head_backward, (query_heads, key_heads, value_heads, attended_hea...  169 us
    unnamed x1, blocking collectives  157 us
    all_to_all x1, blocking collectives, per_device(): lax.all_to_all(query_part.transpose(1, 0, 2), 'seq', split_axis=0, concat...  40.3 us
  transfers between devices with their start and end apart: 6, of which 4 were waited for; matrix products, arithmetic and copies ran while one was open for 2% of the time, Pallas kernels for 0%

commit v1 on v0

v1 whole, which is shorter than its diff:
```python
import functools

import jax
import jax.numpy as jnp
from jax import lax
from jax.experimental import pallas as pl
from jax.experimental.pallas import tpu as pltpu
from jax.sharding import PartitionSpec as P

HEAD_DIM = 128
N_SEQ = 4
Z, Y = 8, 4
EPSILON = 1e-06
SCORE_SCALE = HEAD_DIM ** (-0.5)
MESH = pl.DeviceIdType.MESH
VMEM = pltpu.VMEM


def dp_partner(stage, k):
    d = lax.axis_index("dp")
    if stage == "z":
        return (d // Z) * Z + (d % Z + k) % Z
    if stage == "y":
        row = (d // Z) % Y
        return d + ((row + k) % Y - row) * Z
    return (d + Z * Y) % (2 * Z * Y)


STAGES = (("z", Z - 1), ("y", Y - 1), ("x", 1))


def all_partners():
    s = lax.axis_index("seq")
    found = [{"seq": (s + k) % N_SEQ} for k in range(1, N_SEQ)]
    for stage, count in STAGES:
        found += [{"dp": dp_partner(stage, k)} for k in range(1, count + 1)]
    return found


def enter(partners):
    barrier = pltpu.get_barrier_semaphore()
    for partner in partners:
        pl.semaphore_signal(barrier, inc=1, device_id=partner, device_id_type=MESH)
    pl.semaphore_wait(barrier, len(partners))


def dp_sum(stages, start, bufs, sums, send, recv, base):
    current = start
    for index, (stage, count) in enumerate(stages):
        copies = []
        for k in range(1, count + 1):
            copies.append(
                pltpu.make_async_remote_copy(
                    src_ref=current,
                    dst_ref=bufs[stage].at[k - 1],
                    send_sem=send.at[base],
                    recv_sem=recv.at[base],
                    device_id={"dp": dp_partner(stage, k)},
                    device_id_type=MESH,
                )
            )
            base += 1
            copies[-1].start()
        total = current[...]
        for k, copy in enumerate(copies):
            copy.wait_recv()
            total = total + bufs[stage][k]
        sums[index][...] = total
        for copy in copies:
            copy.wait_send()
        current = sums[index]
    return current


def gather_kernel(x_ref, out_ref, zb, yb, xb, s0, s1, s2, full, send, recv):
    s = lax.axis_index("seq")
    enter(all_partners())
    width = x_ref.shape[1]
    mine = dp_sum(STAGES, x_ref, {"z": zb, "y": yb, "x": xb}, (s0, s1, s2), send, recv, 0)
    base = sum(count for _, count in STAGES)
    copies = []
    for k in range(1, N_SEQ):
        copies.append(
            pltpu.make_async_remote_copy(
                src_ref=mine,
                dst_ref=full.at[s],
                send_sem=send.at[base],
                recv_sem=recv.at[base],
                device_id={"seq": (s + k) % N_SEQ},
                device_id_type=MESH,
            )
        )
        base += 1
        copies[-1].start()
    full[s] = mine[...]
    for copy in copies:
        copy.wait()
    for part in range(N_SEQ):
        out_ref[:, part * width : (part + 1) * width] = full[part]


def stage_scratch(width, extra):
    count = sum(c for _, c in STAGES) + N_SEQ - 1
    return [
        VMEM((Z - 1, 8, width), jnp.float32),
        VMEM((Y - 1, 8, width), jnp.float32),
        VMEM((1, 8, width), jnp.float32),
        VMEM((8, width), jnp.float32),
        VMEM((8, width), jnp.float32),
        VMEM((8, width), jnp.float32),
        *extra,
        pltpu.SemaphoreType.DMA((count,)),
        pltpu.SemaphoreType.DMA((count,)),
    ]


def gather_rows(placed):
    width = placed.shape[1]
    return pl.pallas_call(
        gather_kernel,
        out_shape=jax.ShapeDtypeStruct((8, width * N_SEQ), jnp.float32),
        in_specs=[pl.BlockSpec(memory_space=VMEM)],
        out_specs=pl.BlockSpec(memory_space=VMEM),
        scratch_shapes=stage_scratch(width, [VMEM((N_SEQ, 8, width), jnp.float32)]),
        compiler_params=pltpu.CompilerParams(collective_id=0, has_side_effects=True),
    )(placed)


def reduce_kernel(x_ref, out_ref, zb, yb, xb, s0, s1, s2, first, parts, send, recv):
    s = lax.axis_index("seq")
    width = out_ref.shape[1]
    enter(all_partners())
    copies = []
    for k in range(1, N_SEQ):
        p = (s + k) % N_SEQ
        copies.append(
            pltpu.make_async_remote_copy(
                src_ref=x_ref.at[:, pl.ds(pl.multiple_of(p * width, 128), width)],
                dst_ref=parts.at[k - 1],
                send_sem=send.at[k - 1],
                recv_sem=recv.at[k - 1],
                device_id={"seq": p},
                device_id_type=MESH,
            )
        )
        copies[-1].start()
    total = x_ref[:, pl.ds(pl.multiple_of(s * width, 128), width)]
    for k, copy in enumerate(copies):
        copy.wait_recv()
        total = total + parts[k]
    first[...] = total
    for copy in copies:
        copy.wait_send()
    last = dp_sum(
        STAGES[::-1], first, {"z": zb, "y": yb, "x": xb}, (s0, s1, s2), send, recv, N_SEQ - 1
    )
    out_ref[...] = last[...]


def reduce_rows(rows):
    width = rows.shape[1] // N_SEQ
    return pl.pallas_call(
        reduce_kernel,
        out_shape=jax.ShapeDtypeStruct((8, width), jnp.float32),
        in_specs=[pl.BlockSpec(memory_space=VMEM)],
        out_specs=pl.BlockSpec(memory_space=VMEM),
        scratch_shapes=stage_scratch(
            width, [VMEM((8, width), jnp.float32), VMEM((N_SEQ - 1, 8, width), jnp.float32)]
        ),
        compiler_params=pltpu.CompilerParams(collective_id=1, has_side_effects=True),
    )(rows)


def dot_nt(a, b):
    return lax.dot_general(a, b, (((1,), (1,)), ((), ())), preferred_element_type=jnp.float32)


def dot_nn(a, b):
    return lax.dot_general(a, b, (((1,), (0,)), ((), ())), preferred_element_type=jnp.float32)


BLOCK = 256


def forward_kernel(q_ref, k_ref, v_ref, o_ref, stat_ref):
    keys = k_ref[...]
    values_t = v_ref[...].T

    @pl.loop(0, q_ref.shape[0] // BLOCK)
    def _(i):
        rows = pl.ds(pl.multiple_of(i * BLOCK, BLOCK), BLOCK)
        scores = dot_nt(keys, q_ref[rows, :]) * SCORE_SCALE
        top = jnp.max(scores, axis=0, keepdims=True)
        raised = jnp.exp(scores - top)
        total = jnp.sum(raised, axis=0, keepdims=True)
        weights = (raised * (1.0 / total)).astype(jnp.bfloat16)
        attended_t = dot_nn(values_t, weights)
        o_ref[rows, :] = attended_t.T.astype(jnp.bfloat16)
        stat_ref[0, :, rows] = top + jnp.log(total)


def backward_kernel(q_ref, k_ref, v_ref, o_ref, g_ref, stat_ref, dq_ref, dk_ref, dv_ref):
    keys = k_ref[...]
    keys_t = keys.T
    head_values = v_ref[...]
    dk_ref[...] = jnp.zeros_like(dk_ref)
    dv_ref[...] = jnp.zeros_like(dv_ref)

    @pl.loop(0, q_ref.shape[0] // BLOCK)
    def _(i):
        rows = pl.ds(pl.multiple_of(i * BLOCK, BLOCK), BLOCK)
        queries = q_ref[rows, :]
        grads = g_ref[rows, :]
        scores = dot_nt(keys, queries) * SCORE_SCALE
        weights = jnp.exp(scores - stat_ref[0, :, rows])
        product = grads.astype(jnp.float32) * o_ref[rows, :].astype(jnp.float32)
        row_dot = jnp.sum(product.T, axis=0, keepdims=True)
        weight_grad = dot_nt(head_values, grads)
        score_grad = (weights * (weight_grad - row_dot) * SCORE_SCALE).astype(jnp.bfloat16)
        dv_ref[...] += dot_nn(weights.astype(jnp.bfloat16), grads)
        dk_ref[...] += dot_nn(score_grad, queries)
        dq_ref[rows, :] = dot_nn(keys_t, score_grad).T


def head_spec(rows):
    return pl.BlockSpec((rows, HEAD_DIM), lambda h: (0, h))


def head_forward(q, k, v):
    rows, width = q.shape
    heads = width // HEAD_DIM
    return pl.pallas_call(
        forward_kernel,
        grid=(heads,),
        out_shape=(
            jax.ShapeDtypeStruct((rows, width), jnp.bfloat16),
            jax.ShapeDtypeStruct((heads, 1, rows), jnp.float32),
        ),
        in_specs=[head_spec(rows)] * 3,
        out_specs=(head_spec(rows), pl.BlockSpec((1, 1, rows), lambda h: (h, 0, 0))),
        compiler_params=pltpu.CompilerParams(vmem_limit_bytes=40 << 20),
    )(q, k, v)


def head_backward(q, k, v, o, g, stat):
    rows, width = q.shape
    heads = width // HEAD_DIM
    return pl.pallas_call(
        backward_kernel,
        grid=(heads,),
        out_shape=(jax.ShapeDtypeStruct((rows, width), jnp.float32),) * 3,
        in_specs=[head_spec(rows)] * 5 + [pl.BlockSpec((1, 1, rows), lambda h: (h, 0, 0))],
        out_specs=(head_spec(rows),) * 3,
        compiler_params=pltpu.CompilerParams(vmem_limit_bytes=40 << 20),
    )(q, k, v, o, g, stat)


def root_scale(raw_values):
    floats = raw_values.astype(jnp.float32)
    return lax.rsqrt(jnp.mean(floats * floats, axis=1, keepdims=True) + EPSILON)


def stream_pass(residual, attended, modulated, residual_grad, modulated_grad):
    gate_row = modulated[0]
    scale_row = modulated[1]
    summed = residual.astype(jnp.float32) + gate_row * attended.astype(jnp.float32)
    centered = summed - jnp.mean(summed, axis=1, keepdims=True)
    norm_scale = lax.rsqrt(jnp.mean(centered * centered, axis=1, keepdims=True) + EPSILON)
    normed = centered * norm_scale
    scaled_grad = modulated_grad.astype(jnp.float32) * (1.0 + scale_row)
    stream_grad = residual_grad.astype(jnp.float32) + norm_scale * (
        scaled_grad
        - jnp.mean(scaled_grad, axis=1, keepdims=True)
        - normed * jnp.mean(scaled_grad * normed, axis=1, keepdims=True)
    )
    attended_grad = (stream_grad * gate_row).astype(jnp.bfloat16)
    return (stream_grad, normed, attended_grad)


def norm_backward(raw_values, inverse, gain_row, upstream):
    floats = raw_values.astype(jnp.float32)
    weighted = gain_row * upstream
    return (
        inverse * weighted
        - floats * inverse**3 * jnp.mean(floats * weighted, axis=1, keepdims=True)
    ).astype(jnp.bfloat16)


def to_heads(x):
    return lax.all_to_all(x, "seq", split_axis=1, concat_axis=0, tiled=True)


def to_tokens(x):
    return lax.all_to_all(x, "seq", split_axis=0, concat_axis=1, tiled=True)


def per_device(
    residual,
    query_raw,
    key_raw,
    values,
    residual_grad,
    modulated_grad,
    condition,
    modulation,
    norm_gains,
):
    row_count, width = residual.shape
    own = modulation.shape[1]
    d = lax.axis_index("dp")
    placed = lax.dynamic_update_slice(
        jnp.zeros((8, width // N_SEQ), jnp.float32),
        jnp.concatenate([modulation, norm_gains], axis=0),
        (0, d * own),
    )
    params = gather_rows(placed)
    modulated = params[0:2] + condition[0]
    gains = params[2:4]
    query_scale = root_scale(query_raw)
    key_scale = root_scale(key_raw)
    normed_query = (query_raw.astype(jnp.float32) * query_scale * gains[0]).astype(jnp.bfloat16)
    normed_key = (key_raw.astype(jnp.float32) * key_scale * gains[1]).astype(jnp.bfloat16)
    value_heads = to_heads(values)
    query_heads = to_heads(normed_query)
    key_heads = to_heads(normed_key)
    attended_heads, stat = head_forward(query_heads, key_heads, value_heads)
    attended = to_tokens(attended_heads)
    stream_grad, normed, attended_grad = stream_pass(
        residual, attended, modulated, residual_grad, modulated_grad
    )
    query_part, key_part, value_part = head_backward(
        query_heads, key_heads, value_heads, attended_heads, to_heads(attended_grad), stat
    )
    value_grad = to_tokens(value_part.astype(jnp.bfloat16))
    query_grad_n = to_tokens(query_part.astype(jnp.bfloat16)).astype(jnp.float32)
    key_grad_n = to_tokens(key_part.astype(jnp.bfloat16)).astype(jnp.float32)
    grad_floats = modulated_grad.astype(jnp.float32)
    sums_here = jnp.stack(
        [
            jnp.sum(stream_grad * attended.astype(jnp.float32), axis=0),
            jnp.sum(grad_floats, axis=0),
            jnp.sum(grad_floats * normed, axis=0),
            jnp.sum(query_grad_n * query_raw.astype(jnp.float32) * query_scale, axis=0),
            jnp.sum(key_grad_n * key_raw.astype(jnp.float32) * key_scale, axis=0),
        ]
    )
    reduced = reduce_rows(jnp.pad(sums_here, ((0, 3), (0, 0))))
    factor = (row_count * lax.axis_size("seq") * lax.axis_size("dp")) ** (-0.5)
    return (
        stream_grad.astype(jnp.bfloat16),
        norm_backward(query_raw, query_scale, gains[0], query_grad_n),
        norm_backward(key_raw, key_scale, gains[1], key_grad_n),
        value_grad,
        lax.dynamic_slice(reduced, (0, d * own), (5, own)) * factor,
    )


def solution(mesh):
    rows = P(("seq", "dp"), None)
    columns = P(None, ("seq", "dp"))
    return jax.shard_map(
        per_device,
        mesh=mesh,
        in_specs=(rows,) * 6 + (P("dp", None, None), columns, columns),
        out_specs=(rows,) * 4 + (columns,),
        check_vma=False,
    )
```

time: 1960 us -> 223 us (0.11)
  blocking collectives: 1530 us -> 33.8 us
  local copies, waits for them, and re-layouts: 232 us -> 18.4 us
  Pallas kernels: 0 us -> 73.9 us
  matrix products: 57.8 us -> 0 us
  waiting for transfers between devices: 68.1 us -> 43.9 us
    all_gather x2 -> x0, blocking collectives: 1310 us -> none  [the longest x1 665 us: per_device(): lax.all_gather(modulation, ('seq', 'dp'), axis=1, tiled=True)]
    dynamic_update_slice x20 -> x1, local copies, waits for them, and re-layouts: 176 us -> 0.37 us  [per_device(): lax.dynamic_update_slice(jnp.zeros((8, width // N_SEQ), jnp.float32), jnp...]
    unnamed x1 -> x0, blocking collectives: 157 us -> none
    pallas_call x0 -> x4, Pallas kernels: none -> 73.9 us  [the longest x1 25.5 us: gather_rows(): pl.pallas_call(gather_kernel, out_shape=jax.ShapeDtypeStruct((8, width *...]
    dot_general x35 -> x0, matrix products: 57.8 us -> none  [the longest x10 15 us: head_scores(): lax.dot_general(query_head, key_head, (((1,), (1,)), ((), ())), preferred...]
    all_to_all x2, blocking collectives: 64.8 us -> 33.8 us  [to_heads(): return lax.all_to_all(x, 'seq', split_axis=1, concat_axis=0, tiled=True)]
    all_to_all x6, waiting for transfers between devices: 68.1 us -> 43.9 us  [the longest x4 32 us: to_tokens(): return lax.all_to_all(x, 'seq', split_axis=0, concat_axis=1, tiled=True)]
  transfers between devices with their start and end apart: 6 -> 6, of which waited for: 4 -> 4; matrix products, arithmetic and copies ran while one was open for 2% -> 7% of each run, Pallas kernels for 0% -> 21%
where the time goes in v1:
time: 223 us; the launch traced here: 221 us
  Pallas kernels  73.9 us (33%)
  waiting for transfers between devices  43.9 us (20%)
  blocking collectives  33.8 us (15%)
  starting transfers between devices  30 us (13%)
  other arithmetic  20.1 us (9%)
  local copies, waits for them, and re-layouts  18.4 us (8%)
    all_to_all x2, blocking collectives, to_heads(): return lax.all_to_all(x, 'seq', split_axis=1, concat_axis=0, tiled=True)  33.8 us
    all_to_all x4, waiting for transfers between devices, to_tokens(): return lax.all_to_all(x, 'seq', split_axis=0, concat_axis=1, tiled=True)  32 us
    pallas_call x1, Pallas kernels, gather_rows(): pl.pallas_call(gather_kernel, out_shape=jax.ShapeDtypeStruct((8, width *...  25.5 us
    pallas_call x1, Pallas kernels, reduce_rows(): pl.pallas_call(reduce_kernel, out_shape=jax.ShapeDtypeStruct((8, width),...  21.8 us
    all_to_all x4, starting transfers between devices, to_tokens(): return lax.all_to_all(x, 'seq', split_axis=0, concat_axis=1, tiled=True)  19.3 us
    pallas_call x1, Pallas kernels, head_forward(): pl.pallas_call(forward_kernel, grid=(heads,), out_shape=(jax.ShapeDtypeSt...  13.7 us
    pallas_call x1, Pallas kernels, head_backward(): pl.pallas_call(backward_kernel, grid=(heads,), out_shape=(jax.ShapeDtypeS...  13 us
    all_to_all x2, waiting for transfers between devices, to_heads(): return lax.all_to_all(x, 'seq', split_axis=1, concat_axis=0, tiled=True)  11.9 us
  transfers between devices with their start and end apart: 6, of which 4 were waited for; matrix products, arithmetic and copies ran while one was open for 7% of the time, Pallas kernels for 21%

profile of v1, /device:TPU:1, one launch (start us, length us, event | category | flops | bytes accessed | tf_op | source)
XLA Modules:
  0.0 221.1 jit_solution(5875790393867811710)
XLA Ops:
  0.6 2.3 %copy.35 = bf16[24,4,8,640]{3,2,0,1:T(8,128)(2,1)} copy(bf16[24,4,8,640]{3,2,1,0:T(8,128)(2,1)} %bitcast.71) | data formatting | bytes 1966080 | tf_op jit(solution)/shard_map/all_to_all | solution.py:290
  3.0 6.9 %all-to-all-start.2 = ((bf16[192,4,640]{2,0,1:T(8,128)(2,1)}), bf16[192,4,640]{2,0,1:T(8,128)(2,1)S(1)}, u32[]{:S(2)}, u32[]{:S(2)}) async-start(bf16[192,4,640]{2,0,1:T(8,128)(2,1)} %bitcast.64), calls=%async_computation.2 | async-start | bytes 1966080 | tf_op jit(solution)/shard_map/all_to_all | solution.py:290
  10.4 0.4 dynamic_update_slice.3.x_ref
  10.8 0.6 copy-done.16
  11.4 25.5 %shard_map.128 = f32[8,2560]{1,0:T(8,128)} custom-call(f32[8,640]{1,0:T(8,128)} %copy-done.16), custom_call_target="tpu_custom_call" | custom-call | tf_op jit(solution)/shard_map/pallas_call | solution.py:119
  36.9 1.0 slice_reduce_fusion.1
  37.9 1.3 fusion.10
  39.3 1.0 copy.36
  40.3 3.9 %all-to-all-start.1 = ((bf16[192,4,640]{2,0,1:T(8,128)(2,1)}), bf16[192,4,640]{2,0,1:T(8,128)(2,1)S(1)}, u32[]{:S(2)}, u32[]{:S(2)}) async-start(bf16[192,4,640]{2,0,1:T(8,128)(2,1)} %bitcast.66), calls=%async_computation.1 | async-start | bytes 1966080 | tf_op jit(solution)/shard_map/all_to_all | solution.py:290
  44.2 1.0 copy.37
  45.2 11.9 %all-to-all-done.1 = bf16[192,4,640]{2,0,1:T(8,128)(2,1)S(1)} async-done(((bf16[192,4,640]{2,0,1:T(8,128)(2,1)}), bf16[192,4,640]{2,0,1:T(8,128)(2,1)S(1)}, u32[]{:S(2)}, u32[]{:S(2)}) %all-to-all-start.1) | async-done | bytes 983072 | tf_op jit(solution)/shard_map/all_to_all | solution.py:290
  57.1 17.4 %all_to_all.134 = bf16[192,4,640]{2,0,1:T(8,128)(2,1)S(1)} all-to-all(bf16[192,4,640]{2,0,1:T(8,128)(2,1)} %bitcast.67), channel_id=1, replica_groups=mesh['seq'=4,'dp'=64] {'seq'}, dimensions={1} | all-to-all | bytes 1966080 | tf_op jit(solution)/shard_map/all_to_all | solution.py:290
  74.4 13.7 %shard_map.129 = (bf16[768,640]{1,0:T(8,128)(2,1)S(1)}, f32[5,1,768]{2,1,0:T(1,128)S(1)}) custom-call(bf16[768,640]{1,0:T(8,128)(2,1)S(1)} %bitcast.53, bf16[768,640]{1,0:T(8,128)(2,1)S(1)} %bitcast.51, bf16[768,640]{1,0:T(8,128)(2,1)S(1)} %bitcast.49), custom_call_target="tpu_custom_call" | custom-call | tf_op jit(solution)/shard_map/pallas_call | solution.py:232
  88.1 0.9 copy-done
  89.1 4.9 %all-to-all-start.3 = ((bf16[4,192,640]{2,1,0:T(8,128)(2,1)}), bf16[4,192,640]{2,1,0:T(8,128)(2,1)}, u32[]{:S(2)}, u32[]{:S(2)}) async-start(bf16[4,192,640]{2,1,0:T(8,128)(2,1)} %bitcast.55), calls=%async_computation.3 | async-start | bytes 1966080 | tf_op jit(solution)/shard_map/all_to_all | solution.py:294
  94.0 0.9 bitcast_add_fusion
  94.9 12.0 %all-to-all-done.3 = bf16[4,192,640]{2,1,0:T(8,128)(2,1)} async-done(((bf16[4,192,640]{2,1,0:T(8,128)(2,1)}), bf16[4,192,640]{2,1,0:T(8,128)(2,1)}, u32[]{:S(2)}, u32[]{:S(2)}) %all-to-all-start.3) | async-done | bytes 983072 | tf_op jit(solution)/shard_map/all_to_all | solution.py:294
  107.0 1.3 convert_bitcast_fusion.2
  108.5 1.0 copy-done.14
  109.5 0.4 fusion.28
  110.3 0.8 copy-done.12
  111.1 0.9 fusion.7
  112.0 1.1 multiply_reduce_fusion
  113.2 1.1 multiply_convert_fusion
  114.4 16.4 %all_to_all.135 = bf16[192,4,640]{2,0,1:T(8,128)(2,1)S(1)} all-to-all(bf16[192,4,640]{2,0,1:T(8,128)(2,1)S(1)} %bitcast.70), channel_id=1, replica_groups=mesh['seq'=4,'dp'=64] {'seq'}, dimensions={1} | all-to-all | bytes 1966080 | tf_op jit(solution)/shard_map/all_to_all | solution.py:290
  130.8 13.0 %shard_map.130 = (f32[768,640]{1,0:T(8,128)S(1)}, f32[768,640]{1,0:T(8,128)S(1)}, f32[768,640]{1,0:T(8,128)S(1)}) custom-call(bf16[768,640]{1,0:T(8,128)(2,1)S(1)} %bitcast.54, bf16[768,640]{1,0:T(8,128)(2,1)S(1)} %bitcast.52, bf16[768,640]{1,0:T(8,128)(2,1)S(1)} %bitcast.50, bf16[768,640]{1,0:T(8,128)(2,1)S(1)} %copy-done.1, bf16[768,640]{1,0:T(8,128)(2,1)S(1)} %bitcast.56, ...), custom_call_target="tpu_custom_call" | custom-call | tf_op jit(solution)/shard_map/pallas_call | solution.py:248
  143.8 1.3 copy-done.2
  145.1 1.3 copy-done.4
  146.3 1.0 convert_element_type.91
  147.4 4.2 %all-to-all-start.5 = ((bf16[4,192,640]{2,1,0:T(8,128)(2,1)}), bf16[4,192,640]{2,1,0:T(8,128)(2,1)S(1)}, u32[]{:S(2)}, u32[]{:S(2)}) async-start(bf16[4,192,640]{2,1,0:T(8,128)(2,1)} %bitcast.14), calls=%async_computation.5 | async-start | bytes 1966080 | tf_op jit(solution)/shard_map/all_to_all | solution.py:294
  151.6 2.7 %convert_element_type.96 = bf16[768,640]{1,0:T(8,128)(2,1)} convert(f32[768,640]{1,0:T(8,128)} %copy-done.4) | non-fusion elementwise | flops 491520 | bytes 2949120 | tf_op jit(solution)/shard_map/convert_element_type | solution.py:336
  154.4 10.2 %all-to-all-done.5 = bf16[4,192,640]{2,1,0:T(8,128)(2,1)S(1)} async-done(((bf16[4,192,640]{2,1,0:T(8,128)(2,1)}), bf16[4,192,640]{2,1,0:T(8,128)(2,1)S(1)}, u32[]{:S(2)}, u32[]{:S(2)}) %all-to-all-start.5) | async-done | bytes 983072 | tf_op jit(solution)/shard_map/all_to_all | solution.py:294
  164.5 5.1 %all-to-all-start.6 = ((bf16[4,192,640]{2,1,0:T(8,128)(2,1)}), bf16[4,192,640]{2,1,0:T(8,128)(2,1)}, u32[]{:S(2)}, u32[]{:S(2)}) async-start(bf16[4,192,640]{2,1,0:T(8,128)(2,1)} %bitcast.16), calls=%async_computation.6 | async-start | bytes 1966080 | tf_op jit(solution)/shard_map/all_to_all | solution.py:294
  169.6 1.0 convert_element_type.101
  171.1 1.0 copy-done.8
  172.0 0.7 fusion.16
  172.8 9.8 %all-to-all-done.6 = bf16[4,192,640]{2,1,0:T(8,128)(2,1)} async-done(((bf16[4,192,640]{2,1,0:T(8,128)(2,1)}), bf16[4,192,640]{2,1,0:T(8,128)(2,1)}, u32[]{:S(2)}, u32[]{:S(2)}) %all-to-all-start.6) | async-done | bytes 983072 | tf_op jit(solution)/shard_map/all_to_all | solution.py:294
  182.6 5.1 %all-to-all-start.7 = ((bf16[4,192,640]{2,1,0:T(8,128)(2,1)}), bf16[4,192,640]{2,1,0:T(8,128)(2,1)}, u32[]{:S(2)}, u32[]{:S(2)}) async-start(bf16[4,192,640]{2,1,0:T(8,128)(2,1)} %bitcast.63), calls=%async_computation.7 | async-start | bytes 1966080 | tf_op jit(solution)/shard_map/all_to_all | solution.py:294
  187.7 1.3 convert_bitcast_fusion
  189.2 1.3 copy-done.5
  190.5 0.7 fusion.25
  191.4 0.6 pad.4.x_ref
  192.0 21.8 %shard_map.131 = f32[8,640]{1,0:T(8,128)} custom-call(f32[8,2560]{1,0:T(8,128)} %pad.4.x_ref), custom_call_target="tpu_custom_call" | custom-call | tf_op jit(solution)/shard_map/pallas_call | solution.py:162
  213.8 1.4 dynamic-slice_multiply_fusion
  215.2 2.2 %copy.29 = bf16[4,24,8,640]{3,2,0,1:T(8,128)(2,1)} copy(bf16[4,24,8,640]{3,2,1,0:T(8,128)(2,1)} %bitcast.35) | data formatting | bytes 1966080 | tf_op jit(solution)/shard_map/all_to_all | solution.py:294
  217.5 1.5 fusion.13
  219.1 0.5 copy-done.11
  219.6 1.5 fusion.22
  (58 shorter events, 2.3 us)
Async XLA Ops:
  0.6 9.2 %copy-start.7 = (bf16[192,2560]{1,0:T(8,128)(2,1)S(1)}, bf16[192,2560]{1,0:T(8,128)(2,1)}, u32[]{:S(2)}) copy-start(bf16[192,2560]{1,0:T(8,128)(2,1)} %param.10) | copy-start | bytes 2949124
  3.0 7.1 %copy-start.9 = (bf16[192,2560]{1,0:T(8,128)(2,1)S(1)}, bf16[192,2560]{1,0:T(8,128)(2,1)}, u32[]{:S(2)}) copy-start(bf16[192,2560]{1,0:T(8,128)(2,1)} %param.11) | copy-start | bytes 2949124
  3.0 7.4 %copy-start.18 = (f32[2,10]{1,0:T(2,128)S(1)}, f32[2,10]{1,0:T(2,128)}, u32[]{:S(2)}) copy-start(f32[2,10]{1,0:T(2,128)} %param.17) | copy-start | bytes 244
  3.0 7.4 %copy-start.19 = (f32[2,10]{1,0:T(2,128)S(1)}, f32[2,10]{1,0:T(2,128)}, u32[]{:S(2)}) copy-start(f32[2,10]{1,0:T(2,128)} %param.16) | copy-start | bytes 244
  3.0 37.3 %all-to-all-start.2 = ((bf16[192,4,640]{2,0,1:T(8,128)(2,1)}), bf16[192,4,640]{2,0,1:T(8,128)(2,1)S(1)}, u32[]{:S(2)}, u32[]{:S(2)}) async-start(bf16[192,4,640]{2,0,1:T(8,128)(2,1)} %bitcast.64), calls=%async_computation.2 | async-start | bytes 1966080 | tf_op jit(solution)/shard_map/all_to_all | solution.py:290
  10.8 0.6 copy-start.16
  39.3 4.9 %copy-start.13 = (bf16[192,2560]{1,0:T(8,128)(2,1)S(1)}, bf16[192,2560]{1,0:T(8,128)(2,1)}, u32[]{:S(2)}) copy-start(bf16[192,2560]{1,0:T(8,128)(2,1)} %get-tuple-element.37) | copy-start | bytes 2949124
  40.3 16.8 %all-to-all-start.1 = ((bf16[192,4,640]{2,0,1:T(8,128)(2,1)}), bf16[192,4,640]{2,0,1:T(8,128)(2,1)S(1)}, u32[]{:S(2)}, u32[]{:S(2)}) async-start(bf16[192,4,640]{2,0,1:T(8,128)(2,1)} %bitcast.66), calls=%async_computation.1 | async-start | bytes 1966080 | tf_op jit(solution)/shard_map/all_to_all | solution.py:290
  74.4 19.5 %copy-start.17 = (f32[1,2,2560]{2,1,0:T(2,128)S(1)}, f32[1,2,2560]{2,1,0:T(2,128)}, u32[]{:S(2)}) copy-start(f32[1,2,2560]{2,1,0:T(2,128)} %param.15) | copy-start | bytes 61444
  88.1 0.9 copy-start
  89.1 17.9 %all-to-all-start.3 = ((bf16[4,192,640]{2,1,0:T(8,128)(2,1)}), bf16[4,192,640]{2,1,0:T(8,128)(2,1)}, u32[]{:S(2)}, u32[]{:S(2)}) async-start(bf16[4,192,640]{2,1,0:T(8,128)(2,1)} %bitcast.55), calls=%async_computation.3 | async-start | bytes 1966080 | tf_op jit(solution)/shard_map/all_to_all | solution.py:294
  108.3 1.2 copy-start.14
  109.9 1.2 copy-start.12
  110.2 1.8 copy-start.15
  114.3 16.5 %copy-start.1 = (bf16[768,640]{1,0:T(8,128)(2,1)S(1)}, bf16[768,640]{1,0:T(8,128)(2,1)}, u32[]{:S(2)}) copy-start(bf16[768,640]{1,0:T(8,128)(2,1)} %copy-done) | copy-start | bytes 2949124
  143.8 1.3 copy-start.2
  145.1 1.3 copy-start.4
  147.4 17.1 %all-to-all-start.5 = ((bf16[4,192,640]{2,1,0:T(8,128)(2,1)}), bf16[4,192,640]{2,1,0:T(8,128)(2,1)S(1)}, u32[]{:S(2)}, u32[]{:S(2)}) async-start(bf16[4,192,640]{2,1,0:T(8,128)(2,1)} %bitcast.14), calls=%async_computation.5 | async-start | bytes 1966080 | tf_op jit(solution)/shard_map/all_to_all | solution.py:294
  151.6 18.0 %copy-start.3 = (f32[768,640]{1,0:T(8,128)S(1)}, f32[768,640]{1,0:T(8,128)}, u32[]{:S(2)}) copy-start(f32[768,640]{1,0:T(8,128)} %copy-done.2) | copy-start | bytes 5898244
  164.5 18.1 %all-to-all-start.6 = ((bf16[4,192,640]{2,1,0:T(8,128)(2,1)}), bf16[4,192,640]{2,1,0:T(8,128)(2,1)}, u32[]{:S(2)}, u32[]{:S(2)}) async-start(bf16[4,192,640]{2,1,0:T(8,128)(2,1)} %bitcast.16), calls=%async_computation.6 | async-start | bytes 1966080 | tf_op jit(solution)/shard_map/all_to_all | solution.py:294
  170.8 1.2 copy-start.8
  182.6 32.6 %all-to-all-start.7 = ((bf16[4,192,640]{2,1,0:T(8,128)(2,1)}), bf16[4,192,640]{2,1,0:T(8,128)(2,1)}, u32[]{:S(2)}, u32[]{:S(2)}) async-start(bf16[4,192,640]{2,1,0:T(8,128)(2,1)} %bitcast.63), calls=%async_computation.7 | async-start | bytes 1966080 | tf_op jit(solution)/shard_map/all_to_all | solution.py:294
  189.0 1.5 copy-start.10
  189.2 1.3 copy-start.5
  217.5 1.7 copy-start.6
  217.5 2.1 copy-start.11

commit v2 on v0

v2 whole, which is shorter than its diff:
```python
import functools

import jax
import jax.numpy as jnp
from jax import lax
from jax.experimental import pallas as pl
from jax.experimental.pallas import tpu as pltpu
from jax.sharding import PartitionSpec as P

HEAD_DIM = 128
N_SEQ = 4
EPSILON = 1e-06
SCORE_SCALE = HEAD_DIM ** (-0.5)
MESH = pl.DeviceIdType.MESH
VMEM = pltpu.VMEM
DMA = pltpu.SemaphoreType.DMA
F32 = jnp.float32
BF16 = jnp.bfloat16
BLOCK = 256
CHUNK = 16


def dot_nt(a, b):
    return lax.dot_general(a, b, (((1,), (1,)), ((), ())), preferred_element_type=F32)


def dot_nn(a, b):
    return lax.dot_general(a, b, (((1,), (0,)), ((), ())), preferred_element_type=F32)


def times(start, width):
    return pl.ds(pl.multiple_of(start, width), width)


def kernel(
    layout,
    placed_ref,
    condition_ref,
    residual_hbm,
    query_hbm,
    key_hbm,
    value_hbm,
    residual_grad_hbm,
    modulated_grad_hbm,
    input_grad_hbm,
    query_grad_hbm,
    key_grad_hbm,
    value_grad_hbm,
    sums_ref,
    residual_t,
    query_t,
    key_t,
    residual_grad_t,
    modulated_grad_t,
    attended_t,
    attended_grad_t,
    input_grad_t,
    query_out_t,
    key_out_t,
    scale_t,
    scale_out,
    query_back,
    key_back,
    query_own,
    key_own,
    modulated,
    query_h,
    key_h,
    value_h,
    scale_in,
    scale_h,
    query_n,
    key_n,
    weights_h,
    attended_h,
    grad_h,
    query_grad_h,
    key_grad_h,
    value_grad_h,
    query_total,
    key_total,
    value_total,
    gain_sums,
    zb,
    yb,
    xb,
    gather_sums,
    full,
    zr,
    yr,
    xr,
    reduce_sums,
    columns,
    column_rows,
    seq_parts,
    in_sem,
    own_sem,
    raw_send,
    raw_recv,
    scale_send,
    scale_recv,
    att_send,
    att_recv,
    grad_send,
    grad_recv,
    back_send,
    back_recv,
    gather_send,
    gather_recv,
    reduce_send,
    reduce_recv,
    out_sem,
    value_sem,
):
    n_z, n_y, n_x = layout
    stages = (("z", n_z - 1), ("y", n_y - 1), ("x", n_x - 1))
    dp_count = sum(count for _, count in stages)
    rows, width = residual_t.shape
    heads = query_h.shape[0]
    local = heads * HEAD_DIM
    tokens = query_h.shape[1]
    s = lax.axis_index("seq")
    d = lax.axis_index("dp")
    hops = range(1, N_SEQ)

    def peer(k):
        return (s + k) % N_SEQ

    def sender(k):
        return (s + N_SEQ - k) % N_SEQ

    def dp_partner(stage, k):
        if stage == "z":
            return (d // n_z) * n_z + (d % n_z + k) % n_z
        if stage == "y":
            row = (d // n_z) % n_y
            return d + ((row + k) % n_y - row) * n_z
        return (d + n_z * n_y * k) % (n_z * n_y * n_x)

    def send(src, dst, send_sem, recv_sem, device):
        return pltpu.make_async_remote_copy(
            src_ref=src,
            dst_ref=dst,
            send_sem=send_sem,
            recv_sem=recv_sem,
            device_id=device,
            device_id_type=MESH,
        )

    def head_columns(owner, h):
        return times((owner * heads + h) * HEAD_DIM, HEAD_DIM)

    def token_rows(owner):
        return times(owner * rows, rows)

    raw_hbm = (key_hbm, query_hbm, value_hbm)
    raw_heads = (key_h, query_h, value_h)

    def raw_copy(t, h, k):
        return send(
            raw_hbm[t].at[:, head_columns(peer(k), h)],
            raw_heads[t].at[h, token_rows(s), :],
            raw_send.at[t, h, k - 1],
            raw_recv.at[t, h, k - 1],
            {"seq": peer(k)},
        )

    def own_copy(t, h):
        return pltpu.make_async_copy(
            raw_hbm[t].at[:, head_columns(s, h)],
            raw_heads[t].at[h, token_rows(s), :],
            own_sem.at[t, h],
        )

    def scale_copy(k):
        return send(
            scale_out,
            scale_in.at[s],
            scale_send.at[k - 1],
            scale_recv.at[k - 1],
            {"seq": peer(k)},
        )

    def att_copy(h, k):
        return send(
            attended_h.at[h, token_rows(peer(k)), :],
            attended_t.at[:, head_columns(s, h)],
            att_send.at[h, k - 1],
            att_recv.at[h, k - 1],
            {"seq": peer(k)},
        )

    def grad_copy(h, k):
        return send(
            attended_grad_t.at[:, head_columns(peer(k), h)],
            grad_h.at[h, token_rows(s), :],
            grad_send.at[h, k - 1],
            grad_recv.at[h, k - 1],
            {"seq": peer(k)},
        )

    def back_copy(t, h, k):
        if t == 2:
            src, dst = value_grad_h, value_grad_hbm.at[:, head_columns(s, h)]
        else:
            src = (query_grad_h, key_grad_h)[t]
            dst = (query_back, key_back)[t].at[k - 1, :, times(h * HEAD_DIM, HEAD_DIM)]
        return send(
            src.at[h, token_rows(peer(k)), :],
            dst,
            back_send.at[t, h, k - 1],
            back_recv.at[t, h, k - 1],
            {"seq": peer(k)},
        )

    def value_copy(h):
        return pltpu.make_async_copy(
            value_grad_h.at[h, token_rows(s), :],
            value_grad_hbm.at[:, head_columns(s, h)],
            value_sem.at[h],
        )

    def start_raw(h):
        for t in range(3):
            for k in hops:
                raw_copy(t, h, k).start()

    def dp_sum(order, start, bufs, totals, send_sem, recv_sem, base, beside):
        current = start
        sent = []
        for index, (stage, count) in enumerate(order):
            copies = [
                send(
                    current,
                    bufs[stage].at[k - 1],
                    send_sem.at[base + k - 1],
                    recv_sem.at[base + k - 1],
                    {"dp": dp_partner(stage, k)},
                )
                for k in range(1, count + 1)
            ]
            base += count
            for copy in copies:
                copy.start()
            beside(index)
            total = current[...]
            for k, copy in enumerate(copies):
                copy.wait_recv()
                total = total + bufs[stage][k]
            totals[index] = total
            sent += copies
            current = totals.at[index]
        return current, sent

    inputs = (
        (key_hbm, key_t),
        (query_hbm, query_t),
        (residual_hbm, residual_t),
        (residual_grad_hbm, residual_grad_t),
        (modulated_grad_hbm, modulated_grad_t),
    )
    loads = [
        pltpu.make_async_copy(src, dst, in_sem.at[i]) for i, (src, dst) in enumerate(inputs)
    ]
    for load in loads:
        load.start()
    for t in range(3):
        for h in range(heads):
            own_copy(t, h).start()

    partners = [{"seq": peer(k)} for k in hops]
    for stage, count in stages:
        partners += [{"dp": dp_partner(stage, k)} for k in range(1, count + 1)]
    barrier = pltpu.get_barrier_semaphore()
    for partner in partners:
        pl.semaphore_signal(barrier, inc=1, device_id=partner, device_id_type=MESH)
    pl.semaphore_wait(barrier, len(partners))

    def scales():
        scale_t[:, rows:, :] = jnp.zeros((2, BLOCK - rows, HEAD_DIM), F32)
        for t, source in ((0, key_t), (1, query_t)):
            loads[t].wait()

            @pl.loop(0, rows // CHUNK)
            def _(i):
                at = times(i * CHUNK, CHUNK)
                floats = source[at, :].astype(F32)
                mean = jnp.sum(floats * floats, axis=1, keepdims=True) * (1.0 / width)
                scale_t[t, at, :] = jnp.broadcast_to(
                    lax.rsqrt(mean + EPSILON), (CHUNK, HEAD_DIM)
                )

            scale_out[t] = scale_t[t].T[0:8, :]
        for k in hops:
            scale_copy(k).start()
        scale_in[s] = scale_out[...]

    def beside_gather(index):
        start_raw(index)
        if index == 0:
            scales()

    mine, gather_copies = dp_sum(
        stages,
        placed_ref,
        {"z": zb, "y": yb, "x": xb},
        gather_sums,
        gather_send,
        gather_recv,
        0,
        beside_gather,
    )
    full[s] = mine[...]
    full_copies = [
        send(
            mine,
            full.at[s],
            gather_send.at[dp_count + k - 1],
            gather_recv.at[dp_count + k - 1],
            {"seq": peer(k)},
        )
        for k in hops
    ]
    for copy in full_copies:
        copy.start()
    for h in range(len(stages), heads):
        start_raw(h)

    for k in hops:
        scale_copy(k).wait_recv()
    for owner in range(N_SEQ):
        for t in range(2):
            spread = jnp.broadcast_to(scale_in[owner, t, 0:1, :], (HEAD_DIM, BLOCK)).T
            scale_h[t, owner * rows : (owner + 1) * rows, :] = spread[0:rows, :]

    @pl.loop(0, heads)
    def _(h):
        gain_at = times(h * HEAD_DIM, HEAD_DIM)
        for t in range(3):
            own_copy(t, h).wait()
            for k in hops:
                raw_copy(t, h, k).wait_recv()
        query_n[h] = (query_h[h].astype(F32) * scale_h[1] * mine[2:3, gain_at]).astype(BF16)
        key_n[h] = (key_h[h].astype(F32) * scale_h[0] * mine[3:4, gain_at]).astype(BF16)
        values_t = value_h[h].T

        @pl.loop(0, tokens // BLOCK)
        def _(i):
            at = times(i * BLOCK, BLOCK)
            scores = dot_nt(key_n[h], query_n[h, at, :]) * SCORE_SCALE
            top = jnp.max(scores, axis=0, keepdims=True)
            raised = jnp.exp(scores - top)
            total = jnp.sum(raised, axis=0, keepdims=True)
            weights = raised * (1.0 / total)
            weights_h[h, :, at] = weights
            attended_h[h, at, :] = dot_nn(values_t, weights.astype(BF16)).T.astype(BF16)

        for k in hops:
            att_copy(h, k).start()
        attended_t[:, head_columns(s, h)] = attended_h[h, token_rows(s), :]

    for copy in full_copies:
        copy.wait_recv()
    for part in range(N_SEQ):
        at = slice(part * local, (part + 1) * local)
        modulated[:, at] = full[part, 0:2, :] + condition_ref[:, at]
    for load in loads[2:]:
        load.wait()
    columns[...] = jnp.zeros_like(columns)

    @pl.loop(0, heads)
    def _(h):
        for k in hops:
            att_copy(h, k).wait_recv()

    @pl.loop(0, rows // CHUNK)
    def _(i):
        at = times(i * CHUNK, CHUNK)
        gate_row = modulated[0:1, :]
        attended = attended_t[at, :].astype(F32)
        summed = residual_t[at, :].astype(F32) + gate_row * attended
        centered = summed - jnp.sum(summed, axis=1, keepdims=True) * (1.0 / width)
        norm_scale = lax.rsqrt(
            jnp.sum(centered * centered, axis=1, keepdims=True) * (1.0 / width) + EPSILON
        )
        normed = centered * norm_scale
        upstream = modulated_grad_t[at, :].astype(F32)
        scaled = upstream * (1.0 + modulated[1:2, :])
        stream_grad = residual_grad_t[at, :].astype(F32) + norm_scale * (
            scaled
            - jnp.sum(scaled, axis=1, keepdims=True) * (1.0 / width)
            - normed * (jnp.sum(scaled * normed, axis=1, keepdims=True) * (1.0 / width))
        )
        input_grad_t[at, :] = stream_grad.astype(BF16)
        attended_grad_t[at, :] = (stream_grad * gate_row).astype(BF16)
        for row, term in enumerate((stream_grad * attended, upstream, upstream * normed)):
            columns[row] += term[0:8, :] + term[8:16, :]

    @pl.loop(0, heads)
    def _(h):
        for k in hops:
            grad_copy(h, k).start()
        grad_h[h, token_rows(s), :] = attended_grad_t[:, head_columns(s, h)]

    input_grad_out = pltpu.make_async_copy(input_grad_t, input_grad_hbm, out_sem.at[0])
    input_grad_out.start()
    column_rows[3:8, :] = jnp.zeros((5, width), F32)
    for row in range(3):
        column_rows[row : row + 1, :] = jnp.sum(columns[row], axis=0, keepdims=True)
    seq_copies = [
        send(
            column_rows.at[:, times(peer(k) * local, HEAD_DIM * heads)],
            seq_parts.at[k - 1],
            reduce_send.at[dp_count + k - 1],
            reduce_recv.at[dp_count + k - 1],
            {"seq": peer(k)},
        )
        for k in hops
    ]
    for copy in seq_copies:
        copy.start()
    gain_sums[0:3, :] = column_rows[0:3, times(s * local, HEAD_DIM * heads)]
    gain_sums[5:8, :] = jnp.zeros((3, local), F32)

    @pl.loop(0, heads)
    def _(h):
        for k in hops:
            grad_copy(h, k).wait_recv()
        at_head = times(h * HEAD_DIM, HEAD_DIM)
        keys_t = key_n[h].T
        key_total[...] = jnp.zeros_like(key_total)
        value_total[...] = jnp.zeros_like(value_total)
        gain_sums[3:4, at_head] = jnp.zeros((1, HEAD_DIM), F32)

        @pl.loop(0, tokens // BLOCK)
        def _(i):
            at = times(i * BLOCK, BLOCK)
            queries = query_n[h, at, :]
            grads = grad_h[h, at, :]
            weights = weights_h[h, :, at]
            product = grads.astype(F32) * attended_h[h, at, :].astype(F32)
            row_dot = jnp.sum(product.T, axis=0, keepdims=True)
            weight_grad = dot_nt(value_h[h], grads)
            score_grad = (weights * (weight_grad - row_dot) * SCORE_SCALE).astype(BF16)
            value_total[...] += dot_nn(weights.astype(BF16), grads)
            key_total[...] += dot_nn(score_grad, queries)
            query_grad = dot_nn(keys_t, score_grad).T
            query_total[at, :] = query_grad
            query_grad_h[h, at, :] = query_grad.astype(BF16)
            gain_sums[3:4, at_head] += jnp.sum(
                query_grad * (query_h[h, at, :].astype(F32) * scale_h[1, at, :]),
                axis=0,
                keepdims=True,
            )

        key_grad_h[h] = key_total[...].astype(BF16)
        value_grad_h[h] = value_total[...].astype(BF16)
        gain_sums[4:5, at_head] = jnp.sum(
            key_total[...] * (key_h[h].astype(F32) * scale_h[0]), axis=0, keepdims=True
        )
        for t in range(3):
            for k in hops:
                back_copy(t, h, k).start()
        value_copy(h).start()
        query_own[:, at_head] = query_total[token_rows(s), :]
        key_own[:, at_head] = key_total[token_rows(s), :]

    for k, copy in enumerate(seq_copies):
        copy.wait_recv()
        gain_sums[0:3, :] += seq_parts[k, 0:3, :]
    reduced, reduce_copies = dp_sum(
        stages[::-1],
        gain_sums,
        {"z": zr, "y": yr, "x": xr},
        reduce_sums,
        reduce_send,
        reduce_recv,
        0,
        lambda index: None,
    )
    sums_ref[...] = reduced[...]

    outs = []
    for t, (raw, back, own, out, out_hbm, scale_row, gain_row) in enumerate(
        (
            (query_t, query_back, query_own, query_out_t, query_grad_hbm, 1, 2),
            (key_t, key_back, key_own, key_out_t, key_grad_hbm, 0, 3),
        )
    ):

        @pl.loop(0, heads)
        def _(h):
            for k in hops:
                back_copy(t, h, k).wait_recv()

        @pl.loop(0, rows // CHUNK)
        def _(i):
            at = times(i * CHUNK, CHUNK)
            inverse = scale_t[scale_row, at, 0:1]
            parts = []
            mean = jnp.zeros((CHUNK, 1), F32)
            for k in range(N_SEQ):
                block = sender(k)
                where = times(block * local, HEAD_DIM * heads)
                upstream = own[at, :] if k == 0 else back[k - 1, at, :].astype(F32)
                weighted = full[block, gain_row : gain_row + 1, :] * upstream
                floats = raw[at, where].astype(F32)
                mean = mean + jnp.sum(floats * weighted, axis=1, keepdims=True)
                parts.append((where, weighted, floats))
            factor = inverse * inverse * inverse * (mean * (1.0 / width))
            for where, weighted, floats in parts:
                out[at, where] = (inverse * weighted - floats * factor).astype(BF16)

        outs.append(pltpu.make_async_copy(out, out_hbm, out_sem.at[1 + t]))
        outs[-1].start()

    @pl.loop(0, heads)
    def _(h):
        for t in range(3):
            for k in hops:
                raw_copy(t, h, k).wait_send()
                back_copy(t, h, k).wait_send()
        for k in hops:
            back_copy(2, h, k).wait_recv()
            att_copy(h, k).wait_send()
            grad_copy(h, k).wait_send()
        value_copy(h).wait()

    for k in hops:
        scale_copy(k).wait_send()
    for copy in gather_copies + full_copies + seq_copies + reduce_copies:
        copy.wait_send()
    input_grad_out.wait()
    for out in outs:
        out.wait()


def whole_block(layout, placed, condition, residual, query, key, value, residual_grad, mod_grad):
    rows, width = residual.shape
    local = width // N_SEQ
    heads = local // HEAD_DIM
    tokens = rows * N_SEQ
    n_z, n_y, n_x = layout
    dp_count = n_z + n_y + n_x - 3
    token = VMEM((rows, width), BF16)
    by_head = VMEM((heads, tokens, HEAD_DIM), BF16)

    def stage_bufs():
        return [VMEM((max(n - 1, 1), 8, local), F32) for n in layout]

    hbm = pl.BlockSpec(memory_space=pl.ANY)
    vmem = pl.BlockSpec(memory_space=VMEM)
    big = jax.ShapeDtypeStruct((rows, width), BF16)
    hops = N_SEQ - 1
    return pl.pallas_call(
        functools.partial(kernel, layout),
        out_shape=(big, big, big, big, jax.ShapeDtypeStruct((8, local), F32)),
        in_specs=[vmem, vmem] + [hbm] * 6,
        out_specs=(hbm, hbm, hbm, hbm, vmem),
        scratch_shapes=[
            token,
            token,
            token,
            token,
            token,
            token,
            token,
            token,
            token,
            token,
            VMEM((2, BLOCK, HEAD_DIM), F32),
            VMEM((2, 8, BLOCK), F32),
            VMEM((hops, rows, local), BF16),
            VMEM((hops, rows, local), BF16),
            VMEM((rows, local), F32),
            VMEM((rows, local), F32),
            VMEM((2, width), F32),
            by_head,
            by_head,
            by_head,
            VMEM((N_SEQ, 2, 8, BLOCK), F32),
            VMEM((2, tokens, HEAD_DIM), F32),
            by_head,
            by_head,
            VMEM((heads, tokens, tokens), F32),
            by_head,
            by_head,
            by_head,
            by_head,
            by_head,
            VMEM((tokens, HEAD_DIM), F32),
            VMEM((tokens, HEAD_DIM), F32),
            VMEM((tokens, HEAD_DIM), F32),
            VMEM((8, local), F32),
            *stage_bufs(),
            VMEM((3, 8, local), F32),
            VMEM((N_SEQ, 8, local), F32),
            *stage_bufs(),
            VMEM((3, 8, local), F32),
            VMEM((3, 8, width), F32),
            VMEM((8, width), F32),
            VMEM((hops, 8, local), F32),
            DMA((5,)),
            DMA((3, heads)),
            DMA((3, heads, hops)),
            DMA((3, heads, hops)),
            DMA((hops,)),
            DMA((hops,)),
            DMA((heads, hops)),
            DMA((heads, hops)),
            DMA((heads, hops)),
            DMA((heads, hops)),
            DMA((3, heads, hops)),
            DMA((3, heads, hops)),
            DMA((dp_count + hops,)),
            DMA((dp_count + hops,)),
            DMA((dp_count + hops,)),
            DMA((dp_count + hops,)),
            DMA((3,)),
            DMA((heads,)),
        ],
        compiler_params=pltpu.CompilerParams(
            collective_id=0, has_side_effects=True, vmem_limit_bytes=58 << 20
        ),
    )(placed, condition, residual, query, key, value, residual_grad, mod_grad)


def per_device(
    layout,
    residual,
    query_raw,
    key_raw,
    values,
    residual_grad,
    modulated_grad,
    condition,
    modulation,
    norm_gains,
):
    row_count, width = residual.shape
    own = modulation.shape[1]
    d = lax.axis_index("dp")
    placed = lax.dynamic_update_slice(
        jnp.zeros((8, width // N_SEQ), F32),
        jnp.concatenate([modulation, norm_gains], axis=0),
        (0, d * own),
    )
    input_grad, query_grad, key_grad, value_grad, reduced = whole_block(
        layout,
        placed,
        condition[0],
        residual,
        query_raw,
        key_raw,
        values,
        residual_grad,
        modulated_grad,
    )
    factor = (row_count * lax.axis_size("seq") * lax.axis_size("dp")) ** (-0.5)
    return (
        input_grad,
        query_grad,
        key_grad,
        value_grad,
        lax.dynamic_slice(reduced, (0, d * own), (5, own)) * factor,
    )


def solution(mesh):
    layout = (8, 4, mesh.shape["dp"] // 32) if mesh.shape["dp"] >= 32 else (mesh.shape["dp"], 1, 1)
    rows = P(("seq", "dp"), None)
    columns = P(None, ("seq", "dp"))
    return jax.shard_map(
        functools.partial(per_device, layout),
        mesh=mesh,
        in_specs=(rows,) * 6 + (P("dp", None, None), columns, columns),
        out_specs=(rows,) * 4 + (columns,),
        check_vma=False,
    )
```

time: 1960 us -> 135 us (0.07)
  blocking collectives: 1530 us -> 0 us
  local copies, waits for them, and re-layouts: 232 us -> 8.01 us
  Pallas kernels: 0 us -> 124 us
  waiting for transfers between devices: 68.1 us -> 0 us
  matrix products: 57.8 us -> 0 us
  other arithmetic: 34.3 us -> 1.38 us
  starting transfers between devices: 30.7 us -> 0 us
    all_gather x2 -> x0, blocking collectives: 1310 us -> none  [the longest x1 665 us: per_device(): lax.all_gather(modulation, ('seq', 'dp'), axis=1, tiled=True)]
    dynamic_update_slice x20 -> x1, local copies, waits for them, and re-layouts: 176 us -> 0.37 us  [per_device(): lax.dynamic_update_slice(jnp.zeros((8, width // N_SEQ), F32), jnp.concate...]
    unnamed x1 -> x0, blocking collectives: 157 us -> none
    pallas_call x0 -> x1, Pallas kernels: none -> 124 us  [whole_block(): pl.pallas_call(functools.partial(kernel, layout), out_shape=(big, big, bi...]
    all_to_all x6 -> x0, waiting for transfers between devices: 68.1 us -> none  [the longest x1 25.5 us: per_device(): lax.all_to_all(key_part.transpose(1, 0, 2), 'seq', split_axis=0, concat_a...]
    all_to_all x2 -> x0, blocking collectives: 64.8 us -> none  [the longest x1 40.3 us: per_device(): lax.all_to_all(query_part.transpose(1, 0, 2), 'seq', split_axis=0, concat...]
    dot_general x35 -> x0, matrix products: 57.8 us -> none  [the longest x10 15 us: head_scores(): lax.dot_general(query_head, key_head, (((1,), (1,)), ((), ())), preferred...]
    all_to_all x6 -> x0, starting transfers between devices: 30.7 us -> none  [the longest x1 6.72 us: per_device(): lax.all_to_all(values.reshape(row_count, -1, head_width), 'seq', split_ax...]
  transfers between devices with their start and end apart: 6 -> 0, of which waited for: 4 -> 0; matrix products, arithmetic and copies ran while one was open for 2% -> 0% of each run, Pallas kernels for 0% -> 0%
where the time goes in v2:
time: 135 us
  Pallas kernels  124 us (92%)
  local copies, waits for them, and re-layouts  8.01 us (6%)
  other arithmetic  1.38 us (1%)
    pallas_call x1, Pallas kernels, whole_block(): pl.pallas_call(functools.partial(kernel, layout), out_shape=(big, big, bi...  124 us
    unnamed x16, local copies, waits for them, and re-layouts  7.63 us

profile of v2, /device:TPU:1, one launch (start us, length us, event | category | flops | bytes accessed | tf_op | source)
XLA Modules:
  0.0 134.5 jit_solution(15715480542534869164)
XLA Ops:
  0.6 0.0 copy-start.4
  0.6 0.0 copy-start.5
  0.7 0.7 copy-done.4
  1.3 0.0 copy-done.5
  1.3 0.4 dynamic_update_slice.3.placed_ref
  1.7 0.0 copy-start.3
  1.7 0.6 copy-done.3
  2.3 124.4 %shard_map.128 = (bf16[192,2560]{1,0:T(8,128)(2,1)}, bf16[192,2560]{1,0:T(8,128)(2,1)}, bf16[192,2560]{1,0:T(8,128)(2,1)}, bf16[192,2560]{1,0:T(8,128)(2,1)}, f32[8,640]{1,0:T(8,128)}) custom-call(f32[8,640]{1,0:T(8,128)} %copy-done.3, f32[2,2560]{1,0:T(2,128)} %bitcast.1, bf16[192,2560]{1,0:T(8,128)(2,1)} %residual_hbm.1, bf16[192,2560]{1,0:T(8,128)(2,1)} %query_hbm.1, ...), custom_call_target="tpu_custom_call" | custom-call | tf_op jit(solution)/shard_map/pallas_call | solution.py:555
  126.8 1.4 %dynamic-slice_multiply_fusion = f32[5,10]{1,0:T(8,128)} fusion(f32[8,640]{1,0:T(8,128)} %get-tuple-element.14, s32[]{:T(128)S(6)} %select_n.4), kind=kLoop, calls=%fused_computation | loop fusion | flops 50 | bytes 404 | tf_op jit(solution)/shard_map/mul | solution.py:665
  128.2 0.0 copy-start.2
  128.2 2.3 %copy.19 = bf16[192,2560]{1,0:T(8,128)(2,1)} copy(bf16[192,2560]{1,0:T(8,128)(2,1)} %get-tuple-element.20) | data formatting | bytes 1966080
  130.5 0.0 copy-done.2
  130.5 0.0 copy-start.1
  130.5 0.9 copy.20
  131.4 0.6 copy-done.1
  132.0 0.0 copy-start
  132.0 0.9 copy.21
  133.0 0.6 copy-done
  133.6 0.9 copy.22
  (2 shorter events, 0.0 us)
Async XLA Ops:
  0.6 0.7 copy-start.4
  0.6 0.7 copy-start.5
  1.7 0.6 copy-start.3
  128.2 2.3 %copy-start.2 = (bf16[192,2560]{1,0:T(8,128)(2,1)S(1)}, bf16[192,2560]{1,0:T(8,128)(2,1)}, u32[]{:S(2)}) copy-start(bf16[192,2560]{1,0:T(8,128)(2,1)} %get-tuple-element.21) | copy-start | bytes 2949124
  130.5 1.6 %copy-start.1 = (bf16[192,2560]{1,0:T(8,128)(2,1)S(1)}, bf16[192,2560]{1,0:T(8,128)(2,1)}, u32[]{:S(2)}) copy-start(bf16[192,2560]{1,0:T(8,128)(2,1)} %get-tuple-element.22) | copy-start | bytes 2949124
  132.0 1.6 %copy-start = (bf16[192,2560]{1,0:T(8,128)(2,1)S(1)}, bf16[192,2560]{1,0:T(8,128)(2,1)}, u32[]{:S(2)}) copy-start(bf16[192,2560]{1,0:T(8,128)(2,1)} %get-tuple-element.23) | copy-start | bytes 2949124

commit v3 on v2

--- a/solution.py
+++ b/solution.py
@@ -18,6 +18,9 @@
 BF16 = jnp.bfloat16
 BLOCK = 256
 CHUNK = 16
+PARTS = ((0, 48), (48, 48), (96, 96))
+EARLY = 2
+SPLIT = 2
 
 
 def dot_nt(a, b):
@@ -34,7 +37,8 @@
 
 def kernel(
     layout,
-    placed_ref,
+    modulation_ref,
+    gains_ref,
     condition_ref,
     residual_hbm,
     query_hbm,
@@ -81,6 +85,7 @@
     key_total,
     value_total,
     gain_sums,
+    placed,
     zb,
     yb,
     xb,
@@ -190,12 +195,17 @@
             {"seq": peer(k)},
         )
 
-    def grad_copy(h, k):
+    def part_rows(part):
+        first, count = PARTS[part]
+        return pl.ds(pl.multiple_of(s * rows + first, CHUNK), count)
+
+    def grad_copy(part, h, k):
+        first, count = PARTS[part]
         return send(
-            attended_grad_t.at[:, head_columns(peer(k), h)],
-            grad_h.at[h, token_rows(s), :],
-            grad_send.at[h, k - 1],
-            grad_recv.at[h, k - 1],
+            attended_grad_t.at[pl.ds(first, count), head_columns(peer(k), h)],
+            grad_h.at[h, part_rows(part), :],
+            grad_send.at[part, h, k - 1],
+            grad_recv.at[part, h, k - 1],
             {"seq": peer(k)},
         )
 
@@ -252,6 +262,10 @@
             current = totals.at[index]
         return current, sent
 
+    def start_back(t, h):
+        for k in hops:
+            back_copy(t, h, k).start()
+
     inputs = (
         (key_hbm, key_t),
         (query_hbm, query_t),
@@ -268,6 +282,12 @@
         for h in range(heads):
             own_copy(t, h).start()
 
+    own = modulation_ref.shape[1]
+    placed[...] = jnp.zeros_like(placed)
+    placed[0:2, 0:own] = modulation_ref[...]
+    placed[2:4, 0:own] = gains_ref[...]
+    placed[...] = pltpu.roll(placed[...], d * own, 1)
+
     partners = [{"seq": peer(k)} for k in hops]
     for stage, count in stages:
         partners += [{"dp": dp_partner(stage, k)} for k in range(1, count + 1)]
@@ -302,7 +322,7 @@
 
     mine, gather_copies = dp_sum(
         stages,
-        placed_ref,
+        placed,
         {"z": zb, "y": yb, "x": xb},
         gather_sums,
         gather_send,
@@ -373,34 +393,38 @@
         for k in hops:
             att_copy(h, k).wait_recv()
 
-    @pl.loop(0, rows // CHUNK)
-    def _(i):
-        at = times(i * CHUNK, CHUNK)
-        gate_row = modulated[0:1, :]
-        attended = attended_t[at, :].astype(F32)
-        summed = residual_t[at, :].astype(F32) + gate_row * attended
-        centered = summed - jnp.sum(summed, axis=1, keepdims=True) * (1.0 / width)
-        norm_scale = lax.rsqrt(
-            jnp.sum(centered * centered, axis=1, keepdims=True) * (1.0 / width) + EPSILON
-        )
-        normed = centered * norm_scale
-        upstream = modulated_grad_t[at, :].astype(F32)
-        scaled = upstream * (1.0 + modulated[1:2, :])
-        stream_grad = residual_grad_t[at, :].astype(F32) + norm_scale * (
-            scaled
-            - jnp.sum(scaled, axis=1, keepdims=True) * (1.0 / width)
-            - normed * (jnp.sum(scaled * normed, axis=1, keepdims=True) * (1.0 / width))
-        )
-        input_grad_t[at, :] = stream_grad.astype(BF16)
-        attended_grad_t[at, :] = (stream_grad * gate_row).astype(BF16)
-        for row, term in enumerate((stream_grad * attended, upstream, upstream * normed)):
-            columns[row] += term[0:8, :] + term[8:16, :]
-
-    @pl.loop(0, heads)
-    def _(h):
-        for k in hops:
-            grad_copy(h, k).start()
-        grad_h[h, token_rows(s), :] = attended_grad_t[:, head_columns(s, h)]
+    for part, (first, count) in enumerate(PARTS):
+
+        @pl.loop(first // CHUNK, (first + count) // CHUNK)
+        def _(i):
+            at = times(i * CHUNK, CHUNK)
+            gate_row = modulated[0:1, :]
+            attended = attended_t[at, :].astype(F32)
+            summed = residual_t[at, :].astype(F32) + gate_row * attended
+            centered = summed - jnp.sum(summed, axis=1, keepdims=True) * (1.0 / width)
+            norm_scale = lax.rsqrt(
+                jnp.sum(centered * centered, axis=1, keepdims=True) * (1.0 / width) + EPSILON
+            )
+            normed = centered * norm_scale
+            upstream = modulated_grad_t[at, :].astype(F32)
+            scaled = upstream * (1.0 + modulated[1:2, :])
+            stream_grad = residual_grad_t[at, :].astype(F32) + norm_scale * (
+                scaled
+                - jnp.sum(scaled, axis=1, keepdims=True) * (1.0 / width)
+                - normed * (jnp.sum(scaled * normed, axis=1, keepdims=True) * (1.0 / width))
+            )
+            input_grad_t[at, :] = stream_grad.astype(BF16)
+            attended_grad_t[at, :] = (stream_grad * gate_row).astype(BF16)
+            for row, term in enumerate((stream_grad * attended, upstream, upstream * normed)):
+                columns[row] += term[0:8, :] + term[8:16, :]
+
+        @pl.loop(0, heads)
+        def _(h):
+            for k in hops:
+                grad_copy(part, h, k).start()
+            grad_h[h, part_rows(part), :] = attended_grad_t[
+                first : first + count, head_columns(s, h)
+            ]
 
     input_grad_out = pltpu.make_async_copy(input_grad_t, input_grad_hbm, out_sem.at[0])
     input_grad_out.start()
@@ -424,8 +448,9 @@
 
     @pl.loop(0, heads)
     def _(h):
-        for k in hops:
-            grad_copy(h, k).wait_recv()
+        for part in range(len(PARTS)):
+            for k in hops:
+                grad_copy(part, h, k).wait_recv()
         at_head = times(h * HEAD_DIM, HEAD_DIM)
         keys_t = key_n[h].T
         key_total[...] = jnp.zeros_like(key_total)
@@ -458,12 +483,23 @@
         gain_sums[4:5, at_head] = jnp.sum(
             key_total[...] * (key_h[h].astype(F32) * scale_h[0]), axis=0, keepdims=True
         )
-        for t in range(3):
-            for k in hops:
-                back_copy(t, h, k).start()
+
+        @pl.when(h < EARLY)
+        def _():
+            for t in range(3):
+                start_back(t, h)
+
         value_copy(h).start()
         query_own[:, at_head] = query_total[token_rows(s), :]
         key_own[:, at_head] = key_total[token_rows(s), :]
+
+    late = [(t, h) for h in range(EARLY, heads) for t in range(2)]
+    late += [(2, h) for h in range(EARLY, heads)]
+
+    def beside_reduce(index):
+        per_stage = len(late) // len(stages)
+        for t, h in late[index * per_stage : (index + 1) * per_stage]:
+            start_back(t, h)
 
     for k, copy in enumerate(seq_copies):
         copy.wait_recv()
@@ -476,9 +512,9 @@
         reduce_send,
         reduce_recv,
         0,
-        lambda index: None,
+        beside_reduce,
     )
-    sums_ref[...] = reduced[...]
+    sums_ref[...] = pltpu.roll(reduced[...], local - d * own, 1)
 
     outs = []
     for t, (raw, back, own, out, out_hbm, scale_row, gain_row) in enumerate(
@@ -523,7 +559,8 @@
         for k in hops:
             back_copy(2, h, k).wait_recv()
             att_copy(h, k).wait_send()
-            grad_copy(h, k).wait_send()
+            for part in range(len(PARTS)):
+                grad_copy(part, h, k).wait_send()
         value_copy(h).wait()
 
     for k in hops:
@@ -535,7 +572,7 @@
         out.wait()
 
 
-def whole_block(layout, placed, condition, residual, query, key, value, residual_grad, mod_grad):
+def whole_block(layout, modulation, gains, condition, residual, query, key, value, residual_grad, mod_grad):
     rows, width = residual.shape
     local = width // N_SEQ
     heads = local // HEAD_DIM
@@ -555,7 +592,7 @@
     return pl.pallas_call(
         functools.partial(kernel, layout),
         out_shape=(big, big, big, big, jax.ShapeDtypeStruct((8, local), F32)),
-        in_specs=[vmem, vmem] + [hbm] * 6,
+        in_specs=[vmem] * 3 + [hbm] * 6,
         out_specs=(hbm, hbm, hbm, hbm, vmem),
         scratch_shapes=[
             token,
@@ -591,6 +628,7 @@
             VMEM((tokens, HEAD_DIM), F32),
             VMEM((tokens, HEAD_DIM), F32),
             VMEM((tokens, HEAD_DIM), F32),
+            VMEM((8, local), F32),
             VMEM((8, local), F32),
             *stage_bufs(),
             VMEM((3, 8, local), F32),
@@ -608,8 +646,8 @@
             DMA((hops,)),
             DMA((heads, hops)),
             DMA((heads, hops)),
-            DMA((heads, hops)),
-            DMA((heads, hops)),
+            DMA((len(PARTS), heads, hops)),
+            DMA((len(PARTS), heads, hops)),
             DMA((3, heads, hops)),
             DMA((3, heads, hops)),
             DMA((dp_count + hops,)),
@@ -622,7 +660,44 @@
         compiler_params=pltpu.CompilerParams(
             collective_id=0, has_side_effects=True, vmem_limit_bytes=58 << 20
         ),
-    )(placed, condition, residual, query, key, value, residual_grad, mod_grad)
+    )(modulation, gains, condition, residual, query, key, value, residual_grad, mod_grad)
+
+
+def results_kernel(factor, *refs):
+    sources, sums_ref, targets, params_ref = refs[:4], refs[4], refs[5:9], refs[9]
+    held, in_sem, out_sem = refs[10:]
+    count = sources[0].shape[0] // SPLIT
+    pieces = [(i, pl.ds(j * count, count), i * SPLIT + j) for i in range(4) for j in range(SPLIT)]
+    loads = [
+        pltpu.make_async_copy(sources[i].at[at, :], held.at[i, at, :], in_sem.at[n])
+        for i, at, n in pieces
+    ]
+    stores = [
+        pltpu.make_async_copy(held.at[i, at, :], targets[i].at[at, :], out_sem.at[n])
+        for i, at, n in pieces
+    ]
+    for load in loads:
+        load.start()
+    rows, own = params_ref.shape
+    params_ref[...] = sums_ref[0:rows, 0:own] * factor
+    for load, store in zip(loads, stores):
+        load.wait()
+        store.start()
+    for store in stores:
+        store.wait()
+
+
+def results(factor, own, parts):
+    hbm = pl.BlockSpec(memory_space=pl.ANY)
+    vmem = pl.BlockSpec(memory_space=VMEM)
+    big = [jax.ShapeDtypeStruct(part.shape, part.dtype) for part in parts[:4]]
+    return pl.pallas_call(
+        functools.partial(results_kernel, factor),
+        out_shape=(*big, jax.ShapeDtypeStruct((5, own), F32)),
+        in_specs=[hbm] * 4 + [vmem],
+        out_specs=(*([hbm] * 4), vmem),
+        scratch_shapes=[VMEM((4, *parts[0].shape), BF16), DMA((4 * SPLIT,)), DMA((4 * SPLIT,))],
+    )(*parts)
 
 
 def per_device(
@@ -637,32 +712,22 @@
     modulation,
     norm_gains,
 ):
-    row_count, width = residual.shape
-    own = modulation.shape[1]
-    d = lax.axis_index("dp")
-    placed = lax.dynamic_update_slice(
-        jnp.zeros((8, width // N_SEQ), F32),
-        jnp.concatenate([modulation, norm_gains], axis=0),
-        (0, d * own),
-    )
-    input_grad, query_grad, key_grad, value_grad, reduced = whole_block(
-        layout,
-        placed,
-        condition[0],
-        residual,
-        query_raw,
-        key_raw,
-        values,
-        residual_grad,
-        modulated_grad,
-    )
-    factor = (row_count * lax.axis_size("seq") * lax.axis_size("dp")) ** (-0.5)
-    return (
-        input_grad,
-        query_grad,
-        key_grad,
-        value_grad,
-        lax.dynamic_slice(reduced, (0, d * own), (5, own)) * factor,
+    factor = (residual.shape[0] * lax.axis_size("seq") * lax.axis_size("dp")) ** (-0.5)
+    return results(
+        factor,
+        modulation.shape[1],
+        whole_block(
+            layout,
+            modulation,
+            norm_gains,
+            condition[0],
+            residual,
+            query_raw,
+            key_raw,
+            values,
+            residual_grad,
+            modulated_grad,
+        ),
     )
 
 

time: 135 us -> 111 us (0.82)
  Pallas kernels: 124 us -> 110 us
  local copies, waits for them, and re-layouts: 8.01 us -> 0 us
  other arithmetic: 1.38 us -> 0 us
    pallas_call x1, Pallas kernels: 124 us -> 105 us  [whole_block(): pl.pallas_call(functools.partial(kernel, layout), out_shape=(big, big, bi...]
    unnamed x16 -> x0, local copies, waits for them, and re-layouts: 7.63 us -> none
    pallas_call x0 -> x1, Pallas kernels: none -> 4.63 us  [results(): pl.pallas_call(functools.partial(results_kernel, factor), out_shape=(*big...]
    mul x1 -> x0, other arithmetic: 1.37 us -> none  [per_device(): lax.dynamic_slice(reduced, (0, d * own), (5, own)) * factor]
where the time goes in v3:
time: 111 us
  Pallas kernels  110 us (99%)
    pallas_call x1, Pallas kernels, whole_block(): pl.pallas_call(functools.partial(kernel, layout), out_shape=(big, big, bi...  105 us
    pallas_call x1, Pallas kernels, results(): pl.pallas_call(functools.partial(results_kernel, factor), out_shape=(*big...  4.63 us

profile of v3, /device:TPU:1, one launch (start us, length us, event | category | flops | bytes accessed | tf_op | source)
XLA Modules:
  0.0 110.6 jit_solution(1112324863636026419)
XLA Ops:
  0.6 105.3 %shard_map.128 = (bf16[192,2560]{1,0:T(8,128)(2,1)}, bf16[192,2560]{1,0:T(8,128)(2,1)}, bf16[192,2560]{1,0:T(8,128)(2,1)}, bf16[192,2560]{1,0:T(8,128)(2,1)}, f32[8,640]{1,0:T(8,128)}) custom-call(f32[2,10]{1,0:T(2,128)} %modulation_ref.1, f32[2,10]{1,0:T(2,128)} %gains_ref.1, f32[2,2560]{1,0:T(2,128)} %bitcast.1, bf16[192,2560]{1,0:T(8,128)(2,1)} %residual_hbm.1, ...), custom_call_target="tpu_custom_call" | custom-call | tf_op jit(solution)/shard_map/pallas_call | solution.py:592
  106.0 4.6 %shard_map.129 = (bf16[192,2560]{1,0:T(8,128)(2,1)}, bf16[192,2560]{1,0:T(8,128)(2,1)}, bf16[192,2560]{1,0:T(8,128)(2,1)}, bf16[192,2560]{1,0:T(8,128)(2,1)}, f32[5,10]{1,0:T(8,128)}) custom-call(bf16[192,2560]{1,0:T(8,128)(2,1)} %get-tuple-element.10.refs_0_, bf16[192,2560]{1,0:T(8,128)(2,1)} %get-tuple-element.11.refs_1_, ...), custom_call_target="tpu_custom_call" | custom-call | tf_op jit(solution)/shard_map/pallas_call | solution.py:694

commit v4 on v3

--- a/solution.py
+++ b/solution.py
@@ -85,16 +85,22 @@
     key_total,
     value_total,
     gain_sums,
-    placed,
-    zb,
-    yb,
-    xb,
-    gather_sums,
+    gather_z,
+    gather_y,
+    gather_x,
+    got_z,
+    got_y,
+    got_x,
+    mine,
     full,
-    zr,
-    yr,
-    xr,
-    reduce_sums,
+    reduce_x,
+    reduce_y,
+    reduce_z,
+    back_x,
+    back_y,
+    back_z,
+    total_x,
+    total_y,
     columns,
     column_rows,
     seq_parts,
@@ -120,6 +126,7 @@
     n_z, n_y, n_x = layout
     stages = (("z", n_z - 1), ("y", n_y - 1), ("x", n_x - 1))
     dp_count = sum(count for _, count in stages)
+    own = modulation_ref.shape[1]
     rows, width = residual_t.shape
     heads = query_h.shape[0]
     local = heads * HEAD_DIM
@@ -127,6 +134,8 @@
     s = lax.axis_index("seq")
     d = lax.axis_index("dp")
     hops = range(1, N_SEQ)
+    at_z, at_y, at_x = d % n_z, (d // n_z) % n_y, d // (n_z * n_y)
+    block_y, block_x = own * n_z, own * n_z * n_y
 
     def peer(k):
         return (s + k) % N_SEQ
@@ -235,32 +244,36 @@
             for k in hops:
                 raw_copy(t, h, k).start()
 
-    def dp_sum(order, start, bufs, totals, send_sem, recv_sem, base, beside):
-        current = start
-        sent = []
-        for index, (stage, count) in enumerate(order):
-            copies = [
-                send(
-                    current,
-                    bufs[stage].at[k - 1],
-                    send_sem.at[base + k - 1],
-                    recv_sem.at[base + k - 1],
-                    {"dp": dp_partner(stage, k)},
-                )
-                for k in range(1, count + 1)
-            ]
-            base += count
-            for copy in copies:
-                copy.start()
-            beside(index)
-            total = current[...]
-            for k, copy in enumerate(copies):
-                copy.wait_recv()
-                total = total + bufs[stage][k]
-            totals[index] = total
-            sent += copies
-            current = totals.at[index]
-        return current, sent
+    def exchange(stage, sources, targets, send_sem, recv_sem, base):
+        copies = [
+            send(
+                source,
+                targets.at[k],
+                send_sem.at[base + k],
+                recv_sem.at[base + k],
+                {"dp": dp_partner(stage, k + 1)},
+            )
+            for k, source in enumerate(sources)
+        ]
+        for copy in copies:
+            copy.start()
+        return copies
+
+    def arrived(start, copies, targets):
+        total = start
+        for k, copy in enumerate(copies):
+            copy.wait_recv()
+            total = total + targets[k]
+        return total
+
+    def widened(ref, values, shift):
+        ref[...] = jnp.zeros_like(ref)
+        ref[:, 0 : values.shape[1]] = values
+        ref[...] = pltpu.roll(ref[...], shift, 1)
+
+    def window(values, first, count):
+        lanes = values.shape[1]
+        return pltpu.roll(values, (lanes - first) % lanes, 1)[:, 0:count]
 
     def start_back(t, h):
         for k in hops:
@@ -282,11 +295,10 @@
         for h in range(heads):
             own_copy(t, h).start()
 
-    own = modulation_ref.shape[1]
-    placed[...] = jnp.zeros_like(placed)
-    placed[0:2, 0:own] = modulation_ref[...]
-    placed[2:4, 0:own] = gains_ref[...]
-    placed[...] = pltpu.roll(placed[...], d * own, 1)
+    gather_z[...] = jnp.zeros_like(gather_z)
+    gather_z[0:2, 0:own] = modulation_ref[...]
+    gather_z[2:4, 0:own] = gains_ref[...]
+    gather_z[...] = pltpu.roll(gather_z[...], at_z * own, 1)
 
     partners = [{"seq": peer(k)} for k in hops]
     for stage, count in stages:
@@ -298,6 +310,7 @@
 
     def scales():
         scale_t[:, rows:, :] = jnp.zeros((2, BLOCK - rows, HEAD_DIM), F32)
+        scale_out[...] = jnp.zeros_like(scale_out)
         for t, source in ((0, key_t), (1, query_t)):
             loads[t].wait()
 
@@ -310,30 +323,32 @@
                     lax.rsqrt(mean + EPSILON), (CHUNK, HEAD_DIM)
                 )
 
-            scale_out[t] = scale_t[t].T[0:8, :]
+            scale_out[t : t + 1, :] = scale_t[t].T[0:1, :]
         for k in hops:
             scale_copy(k).start()
         scale_in[s] = scale_out[...]
 
-    def beside_gather(index):
-        start_raw(index)
-        if index == 0:
-            scales()
-
-    mine, gather_copies = dp_sum(
-        stages,
-        placed,
-        {"z": zb, "y": yb, "x": xb},
-        gather_sums,
-        gather_send,
-        gather_recv,
-        0,
-        beside_gather,
-    )
-    full[s] = mine[...]
+    copies_z = exchange(
+        "z", [gather_z] * (n_z - 1), got_z, gather_send, gather_recv, 0
+    )
+    start_raw(0)
+    scales()
+    widened(gather_y, arrived(gather_z[...], copies_z, got_z), at_y * block_y)
+    copies_y = exchange(
+        "y", [gather_y] * (n_y - 1), got_y, gather_send, gather_recv, n_z - 1
+    )
+    start_raw(1)
+    widened(gather_x, arrived(gather_y[...], copies_y, got_y), at_x * block_x)
+    copies_x = exchange(
+        "x", [gather_x] * (n_x - 1), got_x, gather_send, gather_recv, n_z + n_y - 2
+    )
+    start_raw(2)
+    mine[...] = arrived(gather_x[...], copies_x, got_x)
+    gather_copies = copies_z + copies_y + copies_x
+    full[s] = mine[0:4, :]
     full_copies = [
         send(
-            mine,
+            mine.at[0:4, :],
             full.at[s],
             gather_send.at[dp_count + k - 1],
             gather_recv.at[dp_count + k - 1],
@@ -343,14 +358,14 @@
     ]
     for copy in full_copies:
         copy.start()
-    for h in range(len(stages), heads):
+    for h in range(3, heads):
         start_raw(h)
 
     for k in hops:
         scale_copy(k).wait_recv()
     for owner in range(N_SEQ):
         for t in range(2):
-            spread = jnp.broadcast_to(scale_in[owner, t, 0:1, :], (HEAD_DIM, BLOCK)).T
+            spread = jnp.broadcast_to(scale_in[owner, t : t + 1, :], (HEAD_DIM, BLOCK)).T
             scale_h[t, owner * rows : (owner + 1) * rows, :] = spread[0:rows, :]
 
     @pl.loop(0, heads)
@@ -433,7 +448,7 @@
         column_rows[row : row + 1, :] = jnp.sum(columns[row], axis=0, keepdims=True)
     seq_copies = [
         send(
-            column_rows.at[:, times(peer(k) * local, HEAD_DIM * heads)],
+            column_rows.at[0:4, times(peer(k) * local, HEAD_DIM * heads)],
             seq_parts.at[k - 1],
             reduce_send.at[dp_count + k - 1],
             reduce_recv.at[dp_count + k - 1],
@@ -496,25 +511,44 @@
     late = [(t, h) for h in range(EARLY, heads) for t in range(2)]
     late += [(2, h) for h in range(EARLY, heads)]
 
-    def beside_reduce(index):
-        per_stage = len(late) // len(stages)
+    def start_late(index):
+        per_stage = len(late) // 3
         for t, h in late[index * per_stage : (index + 1) * per_stage]:
             start_back(t, h)
 
     for k, copy in enumerate(seq_copies):
         copy.wait_recv()
         gain_sums[0:3, :] += seq_parts[k, 0:3, :]
-    reduced, reduce_copies = dp_sum(
-        stages[::-1],
-        gain_sums,
-        {"z": zr, "y": yr, "x": xr},
-        reduce_sums,
+    sums = gain_sums[...]
+    for k in range(1, n_x):
+        reduce_x[k - 1] = window(sums, (at_x + k) % n_x * block_x, reduce_x.shape[2])
+    copies_x = exchange(
+        "x", [reduce_x.at[k] for k in range(n_x - 1)], back_x, reduce_send, reduce_recv, 0
+    )
+    start_late(0)
+    total_x[...] = arrived(window(sums, at_x * block_x, total_x.shape[1]), copies_x, back_x)
+    sums = total_x[...]
+    for k in range(1, n_y):
+        reduce_y[k - 1] = window(sums, (at_y + k) % n_y * block_y, reduce_y.shape[2])
+    copies_y = exchange(
+        "y", [reduce_y.at[k] for k in range(n_y - 1)], back_y, reduce_send, reduce_recv, n_x - 1
+    )
+    start_late(1)
+    total_y[...] = arrived(window(sums, at_y * block_y, total_y.shape[1]), copies_y, back_y)
+    sums = total_y[...]
+    for k in range(1, n_z):
+        reduce_z[k - 1] = window(sums, (at_z + k) % n_z * own, reduce_z.shape[2])
+    copies_z = exchange(
+        "z",
+        [reduce_z.at[k] for k in range(n_z - 1)],
+        back_z,
         reduce_send,
         reduce_recv,
-        0,
-        beside_reduce,
-    )
-    sums_ref[...] = pltpu.roll(reduced[...], local - d * own, 1)
+        n_x + n_y - 2,
+    )
+    start_late(2)
+    sums_ref[...] = arrived(window(sums, at_z * own, sums_ref.shape[1]), copies_z, back_z)
+    reduce_copies = copies_x + copies_y + copies_z
 
     outs = []
     for t, (raw, back, own, out, out_hbm, scale_row, gain_row) in enumerate(
@@ -582,17 +616,18 @@
     token = VMEM((rows, width), BF16)
     by_head = VMEM((heads, tokens, HEAD_DIM), BF16)
 
-    def stage_bufs():
-        return [VMEM((max(n - 1, 1), 8, local), F32) for n in layout]
-
+    own = modulation.shape[1]
+    wide_own, wide_z, wide_y = (
+        -(-lanes // HEAD_DIM) * HEAD_DIM for lanes in (own, own * n_z, own * n_z * n_y)
+    )
     hbm = pl.BlockSpec(memory_space=pl.ANY)
     vmem = pl.BlockSpec(memory_space=VMEM)
     big = jax.ShapeDtypeStruct((rows, width), BF16)
     hops = N_SEQ - 1
     return pl.pallas_call(
         functools.partial(kernel, layout),
-        out_shape=(big, big, big, big, jax.ShapeDtypeStruct((8, local), F32)),
-        in_specs=[vmem] * 3 + [hbm] * 6,
+        out_shape=(big, big, big, big, jax.ShapeDtypeStruct((8, wide_own), F32)),
+        in_specs=[vmem] * 3 + [pl.BlockSpec(memory_space=pltpu.HBM)] * 6,
         out_specs=(hbm, hbm, hbm, hbm, vmem),
         scratch_shapes=[
             token,
@@ -606,7 +641,7 @@
             token,
             token,
             VMEM((2, BLOCK, HEAD_DIM), F32),
-            VMEM((2, 8, BLOCK), F32),
+            VMEM((8, BLOCK), F32),
             VMEM((hops, rows, local), BF16),
             VMEM((hops, rows, local), BF16),
             VMEM((rows, local), F32),
@@ -615,7 +650,7 @@
             by_head,
             by_head,
             by_head,
-            VMEM((N_SEQ, 2, 8, BLOCK), F32),
+            VMEM((N_SEQ, 8, BLOCK), F32),
             VMEM((2, tokens, HEAD_DIM), F32),
             by_head,
             by_head,
@@ -629,15 +664,25 @@
             VMEM((tokens, HEAD_DIM), F32),
             VMEM((tokens, HEAD_DIM), F32),
             VMEM((8, local), F32),
+            VMEM((8, wide_z), F32),
+            VMEM((8, wide_y), F32),
             VMEM((8, local), F32),
-            *stage_bufs(),
-            VMEM((3, 8, local), F32),
-            VMEM((N_SEQ, 8, local), F32),
-            *stage_bufs(),
-            VMEM((3, 8, local), F32),
+            VMEM((max(n_z - 1, 1), 8, wide_z), F32),
+            VMEM((max(n_y - 1, 1), 8, wide_y), F32),
+            VMEM((max(n_x - 1, 1), 8, local), F32),
+            VMEM((8, local), F32),
+            VMEM((N_SEQ, 4, local), F32),
+            VMEM((max(n_x - 1, 1), 8, wide_y), F32),
+            VMEM((max(n_y - 1, 1), 8, wide_z), F32),
+            VMEM((max(n_z - 1, 1), 8, wide_own), F32),
+            VMEM((max(n_x - 1, 1), 8, wide_y), F32),
+            VMEM((max(n_y - 1, 1), 8, wide_z), F32),
+            VMEM((max(n_z - 1, 1), 8, wide_own), F32),
+            VMEM((8, wide_y), F32),
+            VMEM((8, wide_z), F32),
             VMEM((3, 8, width), F32),
             VMEM((8, width), F32),
-            VMEM((hops, 8, local), F32),
+            VMEM((hops, 4, local), F32),
             DMA((5,)),
             DMA((3, heads)),
             DMA((3, heads, hops)),
@@ -658,45 +703,36 @@
             DMA((heads,)),
         ],
         compiler_params=pltpu.CompilerParams(
-            collective_id=0, has_side_effects=True, vmem_limit_bytes=58 << 20
+            collective_id=0, has_side_effects=True, vmem_limit_bytes=44 << 20
         ),
     )(modulation, gains, condition, residual, query, key, value, residual_grad, mod_grad)
 
 
 def results_kernel(factor, *refs):
-    sources, sums_ref, targets, params_ref = refs[:4], refs[4], refs[5:9], refs[9]
-    held, in_sem, out_sem = refs[10:]
-    count = sources[0].shape[0] // SPLIT
-    pieces = [(i, pl.ds(j * count, count), i * SPLIT + j) for i in range(4) for j in range(SPLIT)]
-    loads = [
-        pltpu.make_async_copy(sources[i].at[at, :], held.at[i, at, :], in_sem.at[n])
-        for i, at, n in pieces
+    sources, sums_ref, targets, params_ref, sem = refs[:4], refs[4], refs[5:9], refs[9], refs[10]
+    copies = [
+        pltpu.make_async_copy(source, target, sem.at[i])
+        for i, (source, target) in enumerate(zip(sources, targets))
     ]
-    stores = [
-        pltpu.make_async_copy(held.at[i, at, :], targets[i].at[at, :], out_sem.at[n])
-        for i, at, n in pieces
-    ]
-    for load in loads:
-        load.start()
+    for copy in copies:
+        copy.start()
     rows, own = params_ref.shape
     params_ref[...] = sums_ref[0:rows, 0:own] * factor
-    for load, store in zip(loads, stores):
-        load.wait()
-        store.start()
-    for store in stores:
-        store.wait()
+    for copy in copies:
+        copy.wait()
 
 
 def results(factor, own, parts):
-    hbm = pl.BlockSpec(memory_space=pl.ANY)
+    hbm = pl.BlockSpec(memory_space=pltpu.HBM)
     vmem = pl.BlockSpec(memory_space=VMEM)
     big = [jax.ShapeDtypeStruct(part.shape, part.dtype) for part in parts[:4]]
     return pl.pallas_call(
         functools.partial(results_kernel, factor),
         out_shape=(*big, jax.ShapeDtypeStruct((5, own), F32)),
-        in_specs=[hbm] * 4 + [vmem],
+        in_specs=[vmem] * 4 + [vmem],
         out_specs=(*([hbm] * 4), vmem),
-        scratch_shapes=[VMEM((4, *parts[0].shape), BF16), DMA((4 * SPLIT,)), DMA((4 * SPLIT,))],
+        scratch_shapes=[DMA((4,))],
+        compiler_params=pltpu.CompilerParams(vmem_limit_bytes=8 << 20),
     )(*parts)
 
 
@@ -712,6 +748,14 @@
     modulation,
     norm_gains,
 ):
+    residual, query_raw, key_raw, values, residual_grad, modulated_grad = (
+        pltpu.with_memory_space_constraint(x, pltpu.HBM)
+        for x in (residual, query_raw, key_raw, values, residual_grad, modulated_grad)
+    )
+    condition, modulation, norm_gains = (
+        pltpu.with_memory_space_constraint(x, pltpu.HBM)
+        for x in (condition[0], modulation, norm_gains)
+    )
     factor = (residual.shape[0] * lax.axis_size("seq") * lax.axis_size("dp")) ** (-0.5)
     return results(
         factor,
@@ -720,7 +764,7 @@
             layout,
             modulation,
             norm_gains,
-            condition[0],
+            condition,
             residual,
             query_raw,
             key_raw,

time: 111 us -> 107 us (0.964)
  Pallas kernels: 110 us -> 106 us
    pallas_call x1, Pallas kernels: 4.63 us -> 2.54 us  [results(): pl.pallas_call(functools.partial(results_kernel, factor), out_shape=(*big...]
    pallas_call x1, Pallas kernels: 105 us -> 103 us  [whole_block(): pl.pallas_call(functools.partial(kernel, layout), out_shape=(big, big, bi...]
where the time goes in v4:
time: 107 us
  Pallas kernels  106 us (99%)
    pallas_call x1, Pallas kernels, whole_block(): pl.pallas_call(functools.partial(kernel, layout), out_shape=(big, big, bi...  103 us
    pallas_call x1, Pallas kernels, results(): pl.pallas_call(functools.partial(results_kernel, factor), out_shape=(*big...  2.54 us

profile of v4, /device:TPU:1, one launch (start us, length us, event | category | flops | bytes accessed | tf_op | source)
XLA Modules:
  0.0 106.6 jit_solution(7462395665150345344)
XLA Ops:
  0.6 103.4 %shard_map.128 = (bf16[192,2560]{1,0:T(8,128)(2,1)S(1)}, bf16[192,2560]{1,0:T(8,128)(2,1)S(1)}, bf16[192,2560]{1,0:T(8,128)(2,1)S(1)}, bf16[192,2560]{1,0:T(8,128)(2,1)S(1)}, f32[8,128]{1,0:T(8,128)S(1)}) custom-call(f32[2,10]{1,0:T(2,128)} %modulation_ref.1, f32[2,10]{1,0:T(2,128)} %gains_ref.1, f32[2,2560]{1,0:T(2,128)} %bitcast.1, ...), custom_call_target="tpu_custom_call" | custom-call | tf_op jit(solution)/shard_map/pallas_call | solution.py:627
  104.0 2.5 %shard_map.129 = (bf16[192,2560]{1,0:T(8,128)(2,1)}, bf16[192,2560]{1,0:T(8,128)(2,1)}, bf16[192,2560]{1,0:T(8,128)(2,1)}, bf16[192,2560]{1,0:T(8,128)(2,1)}, f32[5,10]{1,0:T(8,128)}) custom-call(bf16[192,2560]{1,0:T(8,128)(2,1)S(1)} %get-tuple-element.10.refs_0_, bf16[192,2560]{1,0:T(8,128)(2,1)S(1)} %get-tuple-element.11.refs_1_, ...), custom_call_target="tpu_custom_call" | custom-call | tf_op jit(solution)/shard_map/pallas_call | solution.py:729

commit v5 on v4

--- a/solution.py
+++ b/solution.py
@@ -18,7 +18,7 @@
 BF16 = jnp.bfloat16
 BLOCK = 256
 CHUNK = 16
-PARTS = ((0, 48), (48, 48), (96, 96))
+HALVES = 2
 EARLY = 2
 SPLIT = 2
 
@@ -114,8 +114,12 @@
     att_recv,
     grad_send,
     grad_recv,
+    wide_send,
+    wide_recv,
     back_send,
     back_recv,
+    value_send,
+    value_recv,
     gather_send,
     gather_recv,
     reduce_send,
@@ -134,6 +138,8 @@
     s = lax.axis_index("seq")
     d = lax.axis_index("dp")
     hops = range(1, N_SEQ)
+    part_size = rows // HALVES
+    part_queries = tokens // HALVES
     at_z, at_y, at_x = d % n_z, (d // n_z) % n_y, d // (n_z * n_y)
     block_y, block_x = own * n_z, own * n_z * n_y
 
@@ -167,24 +173,31 @@
     def token_rows(owner):
         return times(owner * rows, rows)
 
-    raw_hbm = (key_hbm, query_hbm, value_hbm)
-    raw_heads = (key_h, query_h, value_h)
+    def part_rows(part):
+        return pl.ds(part * part_size, part_size)
+
+    def query_rows(part, owner):
+        start = part * part_queries + owner * part_size
+        return pl.ds(pl.multiple_of(start, part_size), part_size)
+
+    def raw_refs(t, h, owner):
+        at = head_columns(owner, h)
+        if t in (0, 2):
+            source, target = ((key_hbm, key_h), (value_hbm, value_h))[t // 2]
+            return source.at[:, at], target.at[h, token_rows(s), :]
+        part = t // 2
+        return query_hbm.at[part_rows(part), at], query_h.at[h, query_rows(part, s), :]
 
     def raw_copy(t, h, k):
         return send(
-            raw_hbm[t].at[:, head_columns(peer(k), h)],
-            raw_heads[t].at[h, token_rows(s), :],
+            *raw_refs(t, h, peer(k)),
             raw_send.at[t, h, k - 1],
             raw_recv.at[t, h, k - 1],
             {"seq": peer(k)},
         )
 
     def own_copy(t, h):
-        return pltpu.make_async_copy(
-            raw_hbm[t].at[:, head_columns(s, h)],
-            raw_heads[t].at[h, token_rows(s), :],
-            own_sem.at[t, h],
-        )
+        return pltpu.make_async_copy(*raw_refs(t, h, s), own_sem.at[t, h])
 
     def scale_copy(k):
         return send(
@@ -195,49 +208,67 @@
             {"seq": peer(k)},
         )
 
-    def att_copy(h, k):
+    def att_copy(part, h, k):
         return send(
-            attended_h.at[h, token_rows(peer(k)), :],
-            attended_t.at[:, head_columns(s, h)],
-            att_send.at[h, k - 1],
-            att_recv.at[h, k - 1],
+            attended_h.at[h, query_rows(part, peer(k)), :],
+            attended_t.at[part_rows(part), head_columns(s, h)],
+            att_send.at[part, h, k - 1],
+            att_recv.at[part, h, k - 1],
             {"seq": peer(k)},
         )
 
-    def part_rows(part):
-        first, count = PARTS[part]
-        return pl.ds(pl.multiple_of(s * rows + first, CHUNK), count)
-
-    def grad_copy(part, h, k):
-        first, count = PARTS[part]
+    def grad_copy(part, k):
         return send(
-            attended_grad_t.at[pl.ds(first, count), head_columns(peer(k), h)],
-            grad_h.at[h, part_rows(part), :],
-            grad_send.at[part, h, k - 1],
-            grad_recv.at[part, h, k - 1],
+            attended_grad_t.at[part_rows(part), times(peer(k) * local, HEAD_DIM * heads)],
+            grad_h.at[query_rows(part, s), :],
+            wide_send.at[part, k - 1],
+            wide_recv.at[part, k - 1],
             {"seq": peer(k)},
         )
 
+    def last_grad_copy(h, k):
+        part = HALVES - 1
+        return send(
+            attended_grad_t.at[part_rows(part), head_columns(peer(k), h)],
+            grad_h.at[query_rows(part, s), times(h * HEAD_DIM, HEAD_DIM)],
+            grad_send.at[h, k - 1],
+            grad_recv.at[h, k - 1],
+            {"seq": peer(k)},
+        )
+
     def back_copy(t, h, k):
-        if t == 2:
-            src, dst = value_grad_h, value_grad_hbm.at[:, head_columns(s, h)]
+        at = times(h * HEAD_DIM, HEAD_DIM)
+        if t == 1:
+            source = key_grad_h.at[h, token_rows(peer(k)), :]
+            target = key_back.at[k - 1, :, at]
         else:
-            src = (query_grad_h, key_grad_h)[t]
-            dst = (query_back, key_back)[t].at[k - 1, :, times(h * HEAD_DIM, HEAD_DIM)]
+            source = query_grad_h.at[h, query_rows(t // 2, peer(k)), :]
+            target = query_back.at[k - 1, part_rows(t // 2), at]
         return send(
-            src.at[h, token_rows(peer(k)), :],
-            dst,
+            source,
+            target,
             back_send.at[t, h, k - 1],
             back_recv.at[t, h, k - 1],
             {"seq": peer(k)},
         )
 
-    def value_copy(h):
-        return pltpu.make_async_copy(
-            value_grad_h.at[h, token_rows(s), :],
-            value_grad_hbm.at[:, head_columns(s, h)],
-            value_sem.at[h],
-        )
+    def value_back(h, k, count=1):
+        return send(
+            value_grad_h.at[token_rows(peer(k)), pl.ds(pl.multiple_of(h * HEAD_DIM, HEAD_DIM), count * HEAD_DIM)],
+            value_grad_hbm.at[
+                :,
+                pl.ds(pl.multiple_of((s * heads + h) * HEAD_DIM, HEAD_DIM), count * HEAD_DIM),
+            ],
+            value_send.at[h, k - 1],
+            value_recv.at[h, k - 1],
+            {"seq": peer(k)},
+        )
+
+    value_own = pltpu.make_async_copy(
+        value_grad_h.at[token_rows(s), :],
+        value_grad_hbm.at[:, times(s * local, HEAD_DIM * heads)],
+        value_sem.at[0],
+    )
 
     def start_raw(h):
         for t in range(3):
@@ -289,23 +320,17 @@
     loads = [
         pltpu.make_async_copy(src, dst, in_sem.at[i]) for i, (src, dst) in enumerate(inputs)
     ]
-    for load in loads:
-        load.start()
-    for t in range(3):
-        for h in range(heads):
-            own_copy(t, h).start()
-
-    gather_z[...] = jnp.zeros_like(gather_z)
-    gather_z[0:2, 0:own] = modulation_ref[...]
-    gather_z[2:4, 0:own] = gains_ref[...]
-    gather_z[...] = pltpu.roll(gather_z[...], at_z * own, 1)
-
     partners = [{"seq": peer(k)} for k in hops]
     for stage, count in stages:
         partners += [{"dp": dp_partner(stage, k)} for k in range(1, count + 1)]
     barrier = pltpu.get_barrier_semaphore()
     for partner in partners:
         pl.semaphore_signal(barrier, inc=1, device_id=partner, device_id_type=MESH)
+    gather_z[...] = jnp.zeros_like(gather_z)
+    gather_z[0:2, 0:own] = modulation_ref[...]
+    gather_z[2:4, 0:own] = gains_ref[...]
+    gather_z[...] = pltpu.roll(gather_z[...], at_z * own, 1)
+
     pl.semaphore_wait(barrier, len(partners))
 
     def scales():
@@ -332,6 +357,11 @@
         "z", [gather_z] * (n_z - 1), got_z, gather_send, gather_recv, 0
     )
     start_raw(0)
+    for load in loads:
+        load.start()
+    for t in range(4):
+        for h in range(heads):
+            own_copy(t, h).start()
     scales()
     widened(gather_y, arrived(gather_z[...], copies_z, got_z), at_y * block_y)
     copies_y = exchange(
@@ -360,39 +390,51 @@
         copy.start()
     for h in range(3, heads):
         start_raw(h)
+    for h in range(heads):
+        for k in hops:
+            raw_copy(3, h, k).start()
 
     for k in hops:
         scale_copy(k).wait_recv()
     for owner in range(N_SEQ):
         for t in range(2):
             spread = jnp.broadcast_to(scale_in[owner, t : t + 1, :], (HEAD_DIM, BLOCK)).T
-            scale_h[t, owner * rows : (owner + 1) * rows, :] = spread[0:rows, :]
-
-    @pl.loop(0, heads)
-    def _(h):
-        gain_at = times(h * HEAD_DIM, HEAD_DIM)
-        for t in range(3):
-            own_copy(t, h).wait()
-            for k in hops:
-                raw_copy(t, h, k).wait_recv()
-        query_n[h] = (query_h[h].astype(F32) * scale_h[1] * mine[2:3, gain_at]).astype(BF16)
-        key_n[h] = (key_h[h].astype(F32) * scale_h[0] * mine[3:4, gain_at]).astype(BF16)
-        values_t = value_h[h].T
-
-        @pl.loop(0, tokens // BLOCK)
-        def _(i):
-            at = times(i * BLOCK, BLOCK)
+            if t == 0:
+                scale_h[t, owner * rows : (owner + 1) * rows, :] = spread[0:rows, :]
+            else:
+                for part in range(HALVES):
+                    at = part * part_queries + owner * part_size
+                    scale_h[t, at : at + part_size, :] = spread[
+                        part * part_size : (part + 1) * part_size, :
+                    ]
+
+    for part, sent in ((0, (0, 1, 2)), (1, (3,))):
+        at = slice(part * part_queries, (part + 1) * part_queries)
+
+        @pl.loop(0, heads)
+        def _(h):
+            gain_at = times(h * HEAD_DIM, HEAD_DIM)
+            for t in sent:
+                own_copy(t, h).wait()
+                for k in hops:
+                    raw_copy(t, h, k).wait_recv()
+            query_n[h, at, :] = (
+                query_h[h, at, :].astype(F32) * scale_h[1, at, :] * mine[2:3, gain_at]
+            ).astype(BF16)
+            if part == 0:
+                key_n[h] = (key_h[h].astype(F32) * scale_h[0] * mine[3:4, gain_at]).astype(BF16)
             scores = dot_nt(key_n[h], query_n[h, at, :]) * SCORE_SCALE
             top = jnp.max(scores, axis=0, keepdims=True)
             raised = jnp.exp(scores - top)
             total = jnp.sum(raised, axis=0, keepdims=True)
             weights = raised * (1.0 / total)
             weights_h[h, :, at] = weights
-            attended_h[h, at, :] = dot_nn(values_t, weights.astype(BF16)).T.astype(BF16)
-
-        for k in hops:
-            att_copy(h, k).start()
-        attended_t[:, head_columns(s, h)] = attended_h[h, token_rows(s), :]
+            attended_h[h, at, :] = dot_nn(value_h[h].T, weights.astype(BF16)).T.astype(BF16)
+            for k in hops:
+                att_copy(part, h, k).start()
+            attended_t[part_rows(part), head_columns(s, h)] = attended_h[
+                h, query_rows(part, s), :
+            ]
 
     for copy in full_copies:
         copy.wait_recv()
@@ -403,14 +445,14 @@
         load.wait()
     columns[...] = jnp.zeros_like(columns)
 
-    @pl.loop(0, heads)
-    def _(h):
-        for k in hops:
-            att_copy(h, k).wait_recv()
-
-    for part, (first, count) in enumerate(PARTS):
-
-        @pl.loop(first // CHUNK, (first + count) // CHUNK)
+    for part in range(HALVES):
+
+        @pl.loop(0, heads)
+        def _(h):
+            for k in hops:
+                att_copy(part, h, k).wait_recv()
+
+        @pl.loop(part * part_size // CHUNK, (part + 1) * part_size // CHUNK)
         def _(i):
             at = times(i * CHUNK, CHUNK)
             gate_row = modulated[0:1, :]
@@ -433,13 +475,19 @@
             for row, term in enumerate((stream_grad * attended, upstream, upstream * normed)):
                 columns[row] += term[0:8, :] + term[8:16, :]
 
-        @pl.loop(0, heads)
-        def _(h):
+        if part < HALVES - 1:
             for k in hops:
-                grad_copy(part, h, k).start()
-            grad_h[h, part_rows(part), :] = attended_grad_t[
-                first : first + count, head_columns(s, h)
-            ]
+                grad_copy(part, k).start()
+        else:
+
+            @pl.loop(0, heads)
+            def _(h):
+                for k in hops:
+                    last_grad_copy(h, k).start()
+
+        grad_h[query_rows(part, s), :] = attended_grad_t[
+            part_rows(part), times(s * local, HEAD_DIM * heads)
+        ]
 
     input_grad_out = pltpu.make_async_copy(input_grad_t, input_grad_hbm, out_sem.at[0])
     input_grad_out.start()
@@ -461,11 +509,14 @@
     gain_sums[0:3, :] = column_rows[0:3, times(s * local, HEAD_DIM * heads)]
     gain_sums[5:8, :] = jnp.zeros((3, local), F32)
 
+    for part in range(HALVES - 1):
+        for k in hops:
+            grad_copy(part, k).wait_recv()
+
     @pl.loop(0, heads)
     def _(h):
-        for part in range(len(PARTS)):
-            for k in hops:
-                grad_copy(part, h, k).wait_recv()
+        for k in hops:
+            last_grad_copy(h, k).wait_recv()
         at_head = times(h * HEAD_DIM, HEAD_DIM)
         keys_t = key_n[h].T
         key_total[...] = jnp.zeros_like(key_total)
@@ -476,7 +527,7 @@
         def _(i):
             at = times(i * BLOCK, BLOCK)
             queries = query_n[h, at, :]
-            grads = grad_h[h, at, :]
+            grads = grad_h[at, at_head]
             weights = weights_h[h, :, at]
             product = grads.astype(F32) * attended_h[h, at, :].astype(F32)
             row_dot = jnp.sum(product.T, axis=0, keepdims=True)
@@ -494,7 +545,7 @@
             )
 
         key_grad_h[h] = key_total[...].astype(BF16)
-        value_grad_h[h] = value_total[...].astype(BF16)
+        value_grad_h[:, at_head] = value_total[...].astype(BF16)
         gain_sums[4:5, at_head] = jnp.sum(
             key_total[...] * (key_h[h].astype(F32) * scale_h[0]), axis=0, keepdims=True
         )
@@ -503,17 +554,20 @@
         def _():
             for t in range(3):
                 start_back(t, h)
-
-        value_copy(h).start()
-        query_own[:, at_head] = query_total[token_rows(s), :]
+            for k in hops:
+                value_back(h, k).start()
+
+        for part in range(HALVES):
+            query_own[part_rows(part), at_head] = query_total[query_rows(part, s), :]
         key_own[:, at_head] = key_total[token_rows(s), :]
 
-    late = [(t, h) for h in range(EARLY, heads) for t in range(2)]
-    late += [(2, h) for h in range(EARLY, heads)]
+    value_own.start()
+
+    late = [(t, h) for h in range(EARLY, heads) for t in (0, 2, 1)]
+    middle = (len(late) + 1) // 2
 
     def start_late(index):
-        per_stage = len(late) // 3
-        for t, h in late[index * per_stage : (index + 1) * per_stage]:
+        for t, h in (late[:middle], late[middle:])[index]:
             start_back(t, h)
 
     for k, copy in enumerate(seq_copies):
@@ -546,9 +600,26 @@
         reduce_recv,
         n_x + n_y - 2,
     )
-    start_late(2)
+    for k in hops:
+        value_back(EARLY, k, heads - EARLY).start()
     sums_ref[...] = arrived(window(sums, at_z * own, sums_ref.shape[1]), copies_z, back_z)
     reduce_copies = copies_x + copies_y + copies_z
+
+    @pl.loop(0, heads)
+    def _(h):
+        for k in hops:
+            for t in range(4):
+                raw_copy(t, h, k).wait_send()
+            for part in range(HALVES):
+                att_copy(part, h, k).wait_send()
+            last_grad_copy(h, k).wait_send()
+
+    for k in hops:
+        scale_copy(k).wait_send()
+        for part in range(HALVES - 1):
+            grad_copy(part, k).wait_send()
+    for copy in gather_copies + full_copies + seq_copies:
+        copy.wait_send()
 
     outs = []
     for t, (raw, back, own, out, out_hbm, scale_row, gain_row) in enumerate(
@@ -560,8 +631,9 @@
 
         @pl.loop(0, heads)
         def _(h):
-            for k in hops:
-                back_copy(t, h, k).wait_recv()
+            for piece in ((0, 2), (1,))[t]:
+                for k in hops:
+                    back_copy(piece, h, k).wait_recv()
 
         @pl.loop(0, rows // CHUNK)
         def _(i):
@@ -588,19 +660,15 @@
     def _(h):
         for t in range(3):
             for k in hops:
-                raw_copy(t, h, k).wait_send()
                 back_copy(t, h, k).wait_send()
-        for k in hops:
-            back_copy(2, h, k).wait_recv()
-            att_copy(h, k).wait_send()
-            for part in range(len(PARTS)):
-                grad_copy(part, h, k).wait_send()
-        value_copy(h).wait()
-
+
+    for copy in reduce_copies:
+        copy.wait_send()
+    value_own.wait()
     for k in hops:
-        scale_copy(k).wait_send()
-    for copy in gather_copies + full_copies + seq_copies + reduce_copies:
-        copy.wait_send()
+        for h in range(EARLY):
+            value_back(h, k).wait()
+        value_back(EARLY, k, heads - EARLY).wait()
     input_grad_out.wait()
     for out in outs:
         out.wait()
@@ -656,10 +724,10 @@
             by_head,
             VMEM((heads, tokens, tokens), F32),
             by_head,
+            VMEM((tokens, local), BF16),
             by_head,
             by_head,
-            by_head,
-            by_head,
+            VMEM((tokens, local), BF16),
             VMEM((tokens, HEAD_DIM), F32),
             VMEM((tokens, HEAD_DIM), F32),
             VMEM((tokens, HEAD_DIM), F32),
@@ -684,23 +752,27 @@
             VMEM((8, width), F32),
             VMEM((hops, 4, local), F32),
             DMA((5,)),
-            DMA((3, heads)),
+            DMA((4, heads)),
+            DMA((4, heads, hops)),
+            DMA((4, heads, hops)),
+            DMA((hops,)),
+            DMA((hops,)),
+            DMA((HALVES, heads, hops)),
+            DMA((HALVES, heads, hops)),
+            DMA((heads, hops)),
+            DMA((heads, hops)),
+            DMA((HALVES - 1, hops)),
+            DMA((HALVES - 1, hops)),
             DMA((3, heads, hops)),
             DMA((3, heads, hops)),
-            DMA((hops,)),
-            DMA((hops,)),
-            DMA((heads, hops)),
-            DMA((heads, hops)),
-            DMA((len(PARTS), heads, hops)),
-            DMA((len(PARTS), heads, hops)),
-            DMA((3, heads, hops)),
-            DMA((3, heads, hops)),
+            DMA((EARLY + 1, hops)),
+            DMA((EARLY + 1, hops)),
             DMA((dp_count + hops,)),
             DMA((dp_count + hops,)),
             DMA((dp_count + hops,)),
             DMA((dp_count + hops,)),
             DMA((3,)),
-            DMA((heads,)),
+            DMA((1,)),
         ],
         compiler_params=pltpu.CompilerParams(
             collective_id=0, has_side_effects=True, vmem_limit_bytes=44 << 20

time: 107 us -> 104 us (0.972)
  Pallas kernels: 106 us -> 103 us
    pallas_call x1, Pallas kernels: 103 us -> 101 us  [whole_block(): pl.pallas_call(functools.partial(kernel, layout), out_shape=(big, big, bi...]
where the time goes in v5:
time: 104 us
  Pallas kernels  103 us (99%)
    pallas_call x1, Pallas kernels, whole_block(): pl.pallas_call(functools.partial(kernel, layout), out_shape=(big, big, bi...  101 us
    pallas_call x1, Pallas kernels, results(): pl.pallas_call(functools.partial(results_kernel, factor), out_shape=(*big...  2.54 us

profile of v5, /device:TPU:1, one launch (start us, length us, event | category | flops | bytes accessed | tf_op | source)
XLA Modules:
  0.0 104.1 jit_solution(1190678793817678209)
XLA Ops:
  0.6 100.9 %shard_map.128 = (bf16[192,2560]{1,0:T(8,128)(2,1)S(1)}, bf16[192,2560]{1,0:T(8,128)(2,1)S(1)}, bf16[192,2560]{1,0:T(8,128)(2,1)S(1)}, bf16[192,2560]{1,0:T(8,128)(2,1)S(1)}, f32[8,128]{1,0:T(8,128)S(1)}) custom-call(f32[2,10]{1,0:T(2,128)} %modulation_ref.1, f32[2,10]{1,0:T(2,128)} %gains_ref.1, f32[2,2560]{1,0:T(2,128)} %bitcast.1, ...), custom_call_target="tpu_custom_call" | custom-call | tf_op jit(solution)/shard_map/pallas_call | solution.py:695
  101.6 2.5 %shard_map.129 = (bf16[192,2560]{1,0:T(8,128)(2,1)}, bf16[192,2560]{1,0:T(8,128)(2,1)}, bf16[192,2560]{1,0:T(8,128)(2,1)}, bf16[192,2560]{1,0:T(8,128)(2,1)}, f32[5,10]{1,0:T(8,128)}) custom-call(bf16[192,2560]{1,0:T(8,128)(2,1)S(1)} %get-tuple-element.10.refs_0_, bf16[192,2560]{1,0:T(8,128)(2,1)S(1)} %get-tuple-element.11.refs_1_, ...), custom_call_target="tpu_custom_call" | custom-call | tf_op jit(solution)/shard_map/pallas_call | solution.py:801

commit v6 on v5

--- a/solution.py
+++ b/solution.py
@@ -37,9 +37,9 @@
 
 def kernel(
     layout,
-    modulation_ref,
-    gains_ref,
-    condition_ref,
+    modulation_hbm,
+    gains_hbm,
+    condition_hbm,
     residual_hbm,
     query_hbm,
     key_hbm,
@@ -85,6 +85,9 @@
     key_total,
     value_total,
     gain_sums,
+    modulation_ref,
+    gains_ref,
+    condition_ref,
     gather_z,
     gather_y,
     gather_x,
@@ -132,9 +135,9 @@
     dp_count = sum(count for _, count in stages)
     own = modulation_ref.shape[1]
     rows, width = residual_t.shape
-    heads = query_h.shape[0]
+    heads = key_h.shape[0]
     local = heads * HEAD_DIM
-    tokens = query_h.shape[1]
+    tokens = key_h.shape[1]
     s = lax.axis_index("seq")
     d = lax.axis_index("dp")
     hops = range(1, N_SEQ)
@@ -185,19 +188,39 @@
         if t in (0, 2):
             source, target = ((key_hbm, key_h), (value_hbm, value_h))[t // 2]
             return source.at[:, at], target.at[h, token_rows(s), :]
-        part = t // 2
-        return query_hbm.at[part_rows(part), at], query_h.at[h, query_rows(part, s), :]
+        if t == 1:
+            target = query_h.at[query_rows(0, s), times(h * HEAD_DIM, HEAD_DIM)]
+            return query_hbm.at[part_rows(0), at], target
+        return (
+            query_hbm.at[part_rows(1), times(owner * local, HEAD_DIM * heads)],
+            query_h.at[query_rows(1, s), :],
+        )
 
     def raw_copy(t, h, k):
         return send(
             *raw_refs(t, h, peer(k)),
-            raw_send.at[t, h, k - 1],
-            raw_recv.at[t, h, k - 1],
+            raw_send.at[t],
+            raw_recv.at[t, h],
             {"seq": peer(k)},
         )
 
     def own_copy(t, h):
-        return pltpu.make_async_copy(*raw_refs(t, h, s), own_sem.at[t, h])
+        return pltpu.make_async_copy(*raw_refs(t, h, s), own_sem.at[0])
+
+    def all_of(ref, sem):
+        pltpu.make_async_copy(ref, ref, sem).wait()
+
+    three_rows, three_parts, three_local = 3 * rows, 3 * part_size, 3 * local
+
+    def all_raw(t, h):
+        at = times(h * HEAD_DIM, HEAD_DIM)
+        if t == 1:
+            ref = query_h.at[0:three_parts, at]
+        elif t == 3:
+            ref = query_h.at[0:three_parts, :]
+        else:
+            ref = (key_h, value_h)[t // 2].at[h, 0:three_rows, :]
+        all_of(ref, raw_recv.at[t, h])
 
     def scale_copy(k):
         return send(
@@ -212,8 +235,8 @@
         return send(
             attended_h.at[h, query_rows(part, peer(k)), :],
             attended_t.at[part_rows(part), head_columns(s, h)],
-            att_send.at[part, h, k - 1],
-            att_recv.at[part, h, k - 1],
+            att_send.at[part],
+            att_recv.at[part],
             {"seq": peer(k)},
         )
 
@@ -221,8 +244,8 @@
         return send(
             attended_grad_t.at[part_rows(part), times(peer(k) * local, HEAD_DIM * heads)],
             grad_h.at[query_rows(part, s), :],
-            wide_send.at[part, k - 1],
-            wide_recv.at[part, k - 1],
+            wide_send.at[part],
+            wide_recv.at[part],
             {"seq": peer(k)},
         )
 
@@ -231,24 +254,24 @@
         return send(
             attended_grad_t.at[part_rows(part), head_columns(peer(k), h)],
             grad_h.at[query_rows(part, s), times(h * HEAD_DIM, HEAD_DIM)],
-            grad_send.at[h, k - 1],
-            grad_recv.at[h, k - 1],
+            grad_send.at[0],
+            grad_recv.at[h],
             {"seq": peer(k)},
         )
 
-    def back_copy(t, h, k):
-        at = times(h * HEAD_DIM, HEAD_DIM)
+    def back_copy(t, h, k, count=1):
+        at = pl.ds(pl.multiple_of(h * HEAD_DIM, HEAD_DIM), count * HEAD_DIM)
         if t == 1:
-            source = key_grad_h.at[h, token_rows(peer(k)), :]
+            source = key_grad_h.at[token_rows(peer(k)), at]
             target = key_back.at[k - 1, :, at]
         else:
-            source = query_grad_h.at[h, query_rows(t // 2, peer(k)), :]
+            source = query_grad_h.at[query_rows(t // 2, peer(k)), at]
             target = query_back.at[k - 1, part_rows(t // 2), at]
         return send(
             source,
             target,
-            back_send.at[t, h, k - 1],
-            back_recv.at[t, h, k - 1],
+            back_send.at[t],
+            back_recv.at[t],
             {"seq": peer(k)},
         )
 
@@ -259,8 +282,8 @@
                 :,
                 pl.ds(pl.multiple_of((s * heads + h) * HEAD_DIM, HEAD_DIM), count * HEAD_DIM),
             ],
-            value_send.at[h, k - 1],
-            value_recv.at[h, k - 1],
+            value_send.at[0],
+            value_recv.at[0],
             {"seq": peer(k)},
         )
 
@@ -320,12 +343,26 @@
     loads = [
         pltpu.make_async_copy(src, dst, in_sem.at[i]) for i, (src, dst) in enumerate(inputs)
     ]
+    small = (
+        (modulation_hbm, modulation_ref),
+        (gains_hbm, gains_ref),
+        (condition_hbm, condition_ref),
+    )
+    small_loads = [
+        pltpu.make_async_copy(src, dst, in_sem.at[len(inputs) + i])
+        for i, (src, dst) in enumerate(small)
+    ]
     partners = [{"seq": peer(k)} for k in hops]
     for stage, count in stages:
         partners += [{"dp": dp_partner(stage, k)} for k in range(1, count + 1)]
     barrier = pltpu.get_barrier_semaphore()
     for partner in partners:
         pl.semaphore_signal(barrier, inc=1, device_id=partner, device_id_type=MESH)
+    for load in small_loads:
+        load.start()
+    for load in small_loads:
+        load.wait()
+
     gather_z[...] = jnp.zeros_like(gather_z)
     gather_z[0:2, 0:own] = modulation_ref[...]
     gather_z[2:4, 0:own] = gains_ref[...]
@@ -359,9 +396,10 @@
     start_raw(0)
     for load in loads:
         load.start()
-    for t in range(4):
+    for t in range(3):
         for h in range(heads):
             own_copy(t, h).start()
+    own_copy(3, 0).start()
     scales()
     widened(gather_y, arrived(gather_z[...], copies_z, got_z), at_y * block_y)
     copies_y = exchange(
@@ -390,9 +428,8 @@
         copy.start()
     for h in range(3, heads):
         start_raw(h)
-    for h in range(heads):
-        for k in hops:
-            raw_copy(3, h, k).start()
+    for k in hops:
+        raw_copy(3, 0, k).start()
 
     for k in hops:
         scale_copy(k).wait_recv()
@@ -408,18 +445,20 @@
                         part * part_size : (part + 1) * part_size, :
                     ]
 
-    for part, sent in ((0, (0, 1, 2)), (1, (3,))):
+    for part, sent in ((0, (0, 1, 2)), (1, ())):
         at = slice(part * part_queries, (part + 1) * part_queries)
+        if part == 0:
+            all_of(attended_t.at[:, 0:three_local], own_sem.at[0])
+        else:
+            all_raw(3, 0)
 
         @pl.loop(0, heads)
         def _(h):
             gain_at = times(h * HEAD_DIM, HEAD_DIM)
             for t in sent:
-                own_copy(t, h).wait()
-                for k in hops:
-                    raw_copy(t, h, k).wait_recv()
+                all_raw(t, h)
             query_n[h, at, :] = (
-                query_h[h, at, :].astype(F32) * scale_h[1, at, :] * mine[2:3, gain_at]
+                query_h[at, gain_at].astype(F32) * scale_h[1, at, :] * mine[2:3, gain_at]
             ).astype(BF16)
             if part == 0:
                 key_n[h] = (key_h[h].astype(F32) * scale_h[0] * mine[3:4, gain_at]).astype(BF16)
@@ -446,11 +485,7 @@
     columns[...] = jnp.zeros_like(columns)
 
     for part in range(HALVES):
-
-        @pl.loop(0, heads)
-        def _(h):
-            for k in hops:
-                att_copy(part, h, k).wait_recv()
+        all_of(attended_t.at[part_rows(part), 0:three_local], att_recv.at[part])
 
         @pl.loop(part * part_size // CHUNK, (part + 1) * part_size // CHUNK)
         def _(i):
@@ -510,13 +545,11 @@
     gain_sums[5:8, :] = jnp.zeros((3, local), F32)
 
     for part in range(HALVES - 1):
-        for k in hops:
-            grad_copy(part, k).wait_recv()
+        all_of(grad_h.at[0:three_parts, :], wide_recv.at[part])
 
     @pl.loop(0, heads)
     def _(h):
-        for k in hops:
-            last_grad_copy(h, k).wait_recv()
+        all_of(grad_h.at[0:three_parts, times(h * HEAD_DIM, HEAD_DIM)], grad_recv.at[h])
         at_head = times(h * HEAD_DIM, HEAD_DIM)
         keys_t = key_n[h].T
         key_total[...] = jnp.zeros_like(key_total)
@@ -537,14 +570,14 @@
             key_total[...] += dot_nn(score_grad, queries)
             query_grad = dot_nn(keys_t, score_grad).T
             query_total[at, :] = query_grad
-            query_grad_h[h, at, :] = query_grad.astype(BF16)
+            query_grad_h[at, at_head] = query_grad.astype(BF16)
             gain_sums[3:4, at_head] += jnp.sum(
-                query_grad * (query_h[h, at, :].astype(F32) * scale_h[1, at, :]),
+                query_grad * (query_h[at, at_head].astype(F32) * scale_h[1, at, :]),
                 axis=0,
                 keepdims=True,
             )
 
-        key_grad_h[h] = key_total[...].astype(BF16)
+        key_grad_h[:, at_head] = key_total[...].astype(BF16)
         value_grad_h[:, at_head] = value_total[...].astype(BF16)
         gain_sums[4:5, at_head] = jnp.sum(
             key_total[...] * (key_h[h].astype(F32) * scale_h[0]), axis=0, keepdims=True
@@ -563,12 +596,10 @@
 
     value_own.start()
 
-    late = [(t, h) for h in range(EARLY, heads) for t in (0, 2, 1)]
-    middle = (len(late) + 1) // 2
-
-    def start_late(index):
-        for t, h in (late[:middle], late[middle:])[index]:
-            start_back(t, h)
+    def start_late(pieces):
+        for t in pieces:
+            for k in hops:
+                back_copy(t, EARLY, k, heads - EARLY).start()
 
     for k, copy in enumerate(seq_copies):
         copy.wait_recv()
@@ -579,7 +610,7 @@
     copies_x = exchange(
         "x", [reduce_x.at[k] for k in range(n_x - 1)], back_x, reduce_send, reduce_recv, 0
     )
-    start_late(0)
+    start_late((0, 2))
     total_x[...] = arrived(window(sums, at_x * block_x, total_x.shape[1]), copies_x, back_x)
     sums = total_x[...]
     for k in range(1, n_y):
@@ -587,7 +618,7 @@
     copies_y = exchange(
         "y", [reduce_y.at[k] for k in range(n_y - 1)], back_y, reduce_send, reduce_recv, n_x - 1
     )
-    start_late(1)
+    start_late((1,))
     total_y[...] = arrived(window(sums, at_y * block_y, total_y.shape[1]), copies_y, back_y)
     sums = total_y[...]
     for k in range(1, n_z):
@@ -605,19 +636,15 @@
     sums_ref[...] = arrived(window(sums, at_z * own, sums_ref.shape[1]), copies_z, back_z)
     reduce_copies = copies_x + copies_y + copies_z
 
-    @pl.loop(0, heads)
-    def _(h):
-        for k in hops:
-            for t in range(4):
-                raw_copy(t, h, k).wait_send()
-            for part in range(HALVES):
-                att_copy(part, h, k).wait_send()
-            last_grad_copy(h, k).wait_send()
-
+    for t in range(4):
+        ref = attended_t.at[part_rows(0), 0:three_local] if t % 2 else attended_t.at[:, 0:three_local]
+        all_of(ref, raw_send.at[t])
+    for part in range(HALVES):
+        all_of(attended_t.at[part_rows(0), 0:three_local], att_send.at[part])
+    for sem in [wide_send.at[part] for part in range(HALVES - 1)] + [grad_send.at[0]]:
+        all_of(attended_grad_t.at[part_rows(0), 0:three_local], sem)
     for k in hops:
         scale_copy(k).wait_send()
-        for part in range(HALVES - 1):
-            grad_copy(part, k).wait_send()
     for copy in gather_copies + full_copies + seq_copies:
         copy.wait_send()
 
@@ -629,11 +656,9 @@
         )
     ):
 
-        @pl.loop(0, heads)
-        def _(h):
-            for piece in ((0, 2), (1,))[t]:
-                for k in hops:
-                    back_copy(piece, h, k).wait_recv()
+        for piece in ((0, 2), (1,))[t]:
+            ref = key_back if piece == 1 else query_back.at[:, part_rows(piece // 2), :]
+            all_of(ref, back_recv.at[piece])
 
         @pl.loop(0, rows // CHUNK)
         def _(i):
@@ -656,19 +681,14 @@
         outs.append(pltpu.make_async_copy(out, out_hbm, out_sem.at[1 + t]))
         outs[-1].start()
 
-    @pl.loop(0, heads)
-    def _(h):
-        for t in range(3):
-            for k in hops:
-                back_copy(t, h, k).wait_send()
-
+    for t in range(3):
+        count = three_rows if t == 1 else three_parts
+        all_of(key_grad_h.at[0:count, :], back_send.at[t])
     for copy in reduce_copies:
         copy.wait_send()
     value_own.wait()
-    for k in hops:
-        for h in range(EARLY):
-            value_back(h, k).wait()
-        value_back(EARLY, k, heads - EARLY).wait()
+    all_of(value_grad_h.at[0:three_rows, :], value_send.at[0])
+    all_of(value_grad_hbm.at[:, 0:three_local], value_recv.at[0])
     input_grad_out.wait()
     for out in outs:
         out.wait()
@@ -683,6 +703,7 @@
     dp_count = n_z + n_y + n_x - 3
     token = VMEM((rows, width), BF16)
     by_head = VMEM((heads, tokens, HEAD_DIM), BF16)
+    wide = VMEM((tokens, local), BF16)
 
     own = modulation.shape[1]
     wide_own, wide_z, wide_y = (
@@ -695,7 +716,7 @@
     return pl.pallas_call(
         functools.partial(kernel, layout),
         out_shape=(big, big, big, big, jax.ShapeDtypeStruct((8, wide_own), F32)),
-        in_specs=[vmem] * 3 + [pl.BlockSpec(memory_space=pltpu.HBM)] * 6,
+        in_specs=[pl.BlockSpec(memory_space=pltpu.HBM)] * 9,
         out_specs=(hbm, hbm, hbm, hbm, vmem),
         scratch_shapes=[
             token,
@@ -715,7 +736,7 @@
             VMEM((rows, local), F32),
             VMEM((rows, local), F32),
             VMEM((2, width), F32),
-            by_head,
+            wide,
             by_head,
             by_head,
             VMEM((N_SEQ, 8, BLOCK), F32),
@@ -724,14 +745,17 @@
             by_head,
             VMEM((heads, tokens, tokens), F32),
             by_head,
-            VMEM((tokens, local), BF16),
-            by_head,
-            by_head,
-            VMEM((tokens, local), BF16),
+            wide,
+            wide,
+            wide,
+            wide,
             VMEM((tokens, HEAD_DIM), F32),
             VMEM((tokens, HEAD_DIM), F32),
             VMEM((tokens, HEAD_DIM), F32),
             VMEM((8, local), F32),
+            VMEM(modulation.shape, F32),
+            VMEM(gains.shape, F32),
+            VMEM(condition.shape, F32),
             VMEM((8, wide_z), F32),
             VMEM((8, wide_y), F32),
             VMEM((8, local), F32),
@@ -751,22 +775,22 @@
             VMEM((3, 8, width), F32),
             VMEM((8, width), F32),
             VMEM((hops, 4, local), F32),
-            DMA((5,)),
+            DMA((8,)),
+            DMA((1,)),
+            DMA((4,)),
             DMA((4, heads)),
-            DMA((4, heads, hops)),
-            DMA((4, heads, hops)),
             DMA((hops,)),
             DMA((hops,)),
-            DMA((HALVES, heads, hops)),
-            DMA((HALVES, heads, hops)),
-            DMA((heads, hops)),
-            DMA((heads, hops)),
-            DMA((HALVES - 1, hops)),
-            DMA((HALVES - 1, hops)),
-            DMA((3, heads, hops)),
-            DMA((3, heads, hops)),
-            DMA((EARLY + 1, hops)),
-            DMA((EARLY + 1, hops)),
+            DMA((HALVES,)),
+            DMA((HALVES,)),
+            DMA((1,)),
+            DMA((heads,)),
+            DMA((HALVES - 1,)),
+            DMA((HALVES - 1,)),
+            DMA((3,)),
+            DMA((3,)),
+            DMA((1,)),
+            DMA((1,)),
             DMA((dp_count + hops,)),
             DMA((dp_count + hops,)),
             DMA((dp_count + hops,)),

time: 104 us -> 101 us (0.971)
  Pallas kernels: 103 us -> 100 us
    pallas_call x1, Pallas kernels: 101 us -> 97.6 us  [whole_block(): pl.pallas_call(functools.partial(kernel, layout), out_shape=(big, big, bi...]
where the time goes in v6:
time: 101 us
  Pallas kernels  100 us (99%)
    pallas_call x1, Pallas kernels, whole_block(): pl.pallas_call(functools.partial(kernel, layout), out_shape=(big, big, bi...  97.6 us
    pallas_call x1, Pallas kernels, results(): pl.pallas_call(functools.partial(results_kernel, factor), out_shape=(*big...  2.54 us

profile of v6, /device:TPU:1, one launch (start us, length us, event | category | flops | bytes accessed | tf_op | source)
XLA Modules:
  0.0 100.8 jit_solution(18243097041030979827)
XLA Ops:
  0.6 97.6 %shard_map.128 = (bf16[192,2560]{1,0:T(8,128)(2,1)S(1)}, bf16[192,2560]{1,0:T(8,128)(2,1)S(1)}, bf16[192,2560]{1,0:T(8,128)(2,1)S(1)}, bf16[192,2560]{1,0:T(8,128)(2,1)S(1)}, f32[8,128]{1,0:T(8,128)S(1)}) custom-call(f32[2,10]{1,0:T(2,128)} %modulation_hbm.1, f32[2,10]{1,0:T(2,128)} %gains_hbm.1, f32[2,2560]{1,0:T(2,128)} %bitcast.1, ...), custom_call_target="tpu_custom_call" | custom-call | tf_op jit(solution)/shard_map/pallas_call | solution.py:716
  98.3 2.5 %shard_map.129 = (bf16[192,2560]{1,0:T(8,128)(2,1)}, bf16[192,2560]{1,0:T(8,128)(2,1)}, bf16[192,2560]{1,0:T(8,128)(2,1)}, bf16[192,2560]{1,0:T(8,128)(2,1)}, f32[5,10]{1,0:T(8,128)}) custom-call(bf16[192,2560]{1,0:T(8,128)(2,1)S(1)} %get-tuple-element.10.refs_0_, bf16[192,2560]{1,0:T(8,128)(2,1)S(1)} %get-tuple-element.11.refs_1_, ...), custom_call_target="tpu_custom_call" | custom-call | tf_op jit(solution)/shard_map/pallas_call | solution.py:825

commit v7 on v6

--- a/solution.py
+++ b/solution.py
@@ -132,7 +132,6 @@
 ):
     n_z, n_y, n_x = layout
     stages = (("z", n_z - 1), ("y", n_y - 1), ("x", n_x - 1))
-    dp_count = sum(count for _, count in stages)
     own = modulation_ref.shape[1]
     rows, width = residual_t.shape
     heads = key_h.shape[0]
@@ -226,8 +225,8 @@
         return send(
             scale_out,
             scale_in.at[s],
-            scale_send.at[k - 1],
-            scale_recv.at[k - 1],
+            scale_send.at[0],
+            scale_recv.at[0],
             {"seq": peer(k)},
         )
 
@@ -298,27 +297,24 @@
             for k in hops:
                 raw_copy(t, h, k).start()
 
-    def exchange(stage, sources, targets, send_sem, recv_sem, base):
-        copies = [
+    def exchange(stage, sources, targets, send_sem, recv_sem):
+        for k, source in enumerate(sources):
             send(
-                source,
-                targets.at[k],
-                send_sem.at[base + k],
-                recv_sem.at[base + k],
-                {"dp": dp_partner(stage, k + 1)},
-            )
-            for k, source in enumerate(sources)
-        ]
-        for copy in copies:
-            copy.start()
-        return copies
-
-    def arrived(start, copies, targets):
+                source, targets.at[k], send_sem, recv_sem, {"dp": dp_partner(stage, k + 1)}
+            ).start()
+        return [(targets, send_sem, recv_sem)] if sources else []
+
+    def arrived(start, group):
         total = start
-        for k, copy in enumerate(copies):
-            copy.wait_recv()
-            total = total + targets[k]
+        for targets, _, recv_sem in group:
+            all_of(targets, recv_sem)
+            for k in range(targets.shape[0]):
+                total = total + targets[k]
         return total
+
+    def sent(groups):
+        for targets, send_sem, _ in groups:
+            all_of(targets, send_sem)
 
     def widened(ref, values, shift):
         ref[...] = jnp.zeros_like(ref)
@@ -391,7 +387,7 @@
         scale_in[s] = scale_out[...]
 
     copies_z = exchange(
-        "z", [gather_z] * (n_z - 1), got_z, gather_send, gather_recv, 0
+        "z", [gather_z] * (n_z - 1), got_z, gather_send.at[0], gather_recv.at[0]
     )
     start_raw(0)
     for load in loads:
@@ -401,25 +397,25 @@
             own_copy(t, h).start()
     own_copy(3, 0).start()
     scales()
-    widened(gather_y, arrived(gather_z[...], copies_z, got_z), at_y * block_y)
+    widened(gather_y, arrived(gather_z[...], copies_z), at_y * block_y)
     copies_y = exchange(
-        "y", [gather_y] * (n_y - 1), got_y, gather_send, gather_recv, n_z - 1
+        "y", [gather_y] * (n_y - 1), got_y, gather_send.at[1], gather_recv.at[1]
     )
     start_raw(1)
-    widened(gather_x, arrived(gather_y[...], copies_y, got_y), at_x * block_x)
+    widened(gather_x, arrived(gather_y[...], copies_y), at_x * block_x)
     copies_x = exchange(
-        "x", [gather_x] * (n_x - 1), got_x, gather_send, gather_recv, n_z + n_y - 2
+        "x", [gather_x] * (n_x - 1), got_x, gather_send.at[2], gather_recv.at[2]
     )
     start_raw(2)
-    mine[...] = arrived(gather_x[...], copies_x, got_x)
+    mine[...] = arrived(gather_x[...], copies_x)
     gather_copies = copies_z + copies_y + copies_x
     full[s] = mine[0:4, :]
     full_copies = [
         send(
             mine.at[0:4, :],
             full.at[s],
-            gather_send.at[dp_count + k - 1],
-            gather_recv.at[dp_count + k - 1],
+            gather_send.at[3],
+            gather_recv.at[3],
             {"seq": peer(k)},
         )
         for k in hops
@@ -431,8 +427,7 @@
     for k in hops:
         raw_copy(3, 0, k).start()
 
-    for k in hops:
-        scale_copy(k).wait_recv()
+    all_of(scale_in.at[0:3], scale_recv.at[0])
     for owner in range(N_SEQ):
         for t in range(2):
             spread = jnp.broadcast_to(scale_in[owner, t : t + 1, :], (HEAD_DIM, BLOCK)).T
@@ -445,7 +440,7 @@
                         part * part_size : (part + 1) * part_size, :
                     ]
 
-    for part, sent in ((0, (0, 1, 2)), (1, ())):
+    for part, pieces in ((0, (0, 1, 2)), (1, ())):
         at = slice(part * part_queries, (part + 1) * part_queries)
         if part == 0:
             all_of(attended_t.at[:, 0:three_local], own_sem.at[0])
@@ -455,7 +450,7 @@
         @pl.loop(0, heads)
         def _(h):
             gain_at = times(h * HEAD_DIM, HEAD_DIM)
-            for t in sent:
+            for t in pieces:
                 all_raw(t, h)
             query_n[h, at, :] = (
                 query_h[at, gain_at].astype(F32) * scale_h[1, at, :] * mine[2:3, gain_at]
@@ -475,8 +470,7 @@
                 h, query_rows(part, s), :
             ]
 
-    for copy in full_copies:
-        copy.wait_recv()
+    all_of(full.at[0:3], gather_recv.at[3])
     for part in range(N_SEQ):
         at = slice(part * local, (part + 1) * local)
         modulated[:, at] = full[part, 0:2, :] + condition_ref[:, at]
@@ -533,8 +527,8 @@
         send(
             column_rows.at[0:4, times(peer(k) * local, HEAD_DIM * heads)],
             seq_parts.at[k - 1],
-            reduce_send.at[dp_count + k - 1],
-            reduce_recv.at[dp_count + k - 1],
+            reduce_send.at[3],
+            reduce_recv.at[3],
             {"seq": peer(k)},
         )
         for k in hops
@@ -601,25 +595,25 @@
             for k in hops:
                 back_copy(t, EARLY, k, heads - EARLY).start()
 
-    for k, copy in enumerate(seq_copies):
-        copy.wait_recv()
+    all_of(seq_parts, reduce_recv.at[3])
+    for k in range(N_SEQ - 1):
         gain_sums[0:3, :] += seq_parts[k, 0:3, :]
     sums = gain_sums[...]
     for k in range(1, n_x):
         reduce_x[k - 1] = window(sums, (at_x + k) % n_x * block_x, reduce_x.shape[2])
     copies_x = exchange(
-        "x", [reduce_x.at[k] for k in range(n_x - 1)], back_x, reduce_send, reduce_recv, 0
+        "x", [reduce_x.at[k] for k in range(n_x - 1)], back_x, reduce_send.at[0], reduce_recv.at[0]
     )
     start_late((0, 2))
-    total_x[...] = arrived(window(sums, at_x * block_x, total_x.shape[1]), copies_x, back_x)
+    total_x[...] = arrived(window(sums, at_x * block_x, total_x.shape[1]), copies_x)
     sums = total_x[...]
     for k in range(1, n_y):
         reduce_y[k - 1] = window(sums, (at_y + k) % n_y * block_y, reduce_y.shape[2])
     copies_y = exchange(
-        "y", [reduce_y.at[k] for k in range(n_y - 1)], back_y, reduce_send, reduce_recv, n_x - 1
+        "y", [reduce_y.at[k] for k in range(n_y - 1)], back_y, reduce_send.at[1], reduce_recv.at[1]
     )
     start_late((1,))
-    total_y[...] = arrived(window(sums, at_y * block_y, total_y.shape[1]), copies_y, back_y)
+    total_y[...] = arrived(window(sums, at_y * block_y, total_y.shape[1]), copies_y)
     sums = total_y[...]
     for k in range(1, n_z):
         reduce_z[k - 1] = window(sums, (at_z + k) % n_z * own, reduce_z.shape[2])
@@ -627,13 +621,12 @@
         "z",
         [reduce_z.at[k] for k in range(n_z - 1)],
         back_z,
-        reduce_send,
-        reduce_recv,
-        n_x + n_y - 2,
+        reduce_send.at[2],
+        reduce_recv.at[2],
     )
     for k in hops:
         value_back(EARLY, k, heads - EARLY).start()
-    sums_ref[...] = arrived(window(sums, at_z * own, sums_ref.shape[1]), copies_z, back_z)
+    sums_ref[...] = arrived(window(sums, at_z * own, sums_ref.shape[1]), copies_z)
     reduce_copies = copies_x + copies_y + copies_z
 
     for t in range(4):
@@ -643,10 +636,10 @@
         all_of(attended_t.at[part_rows(0), 0:three_local], att_send.at[part])
     for sem in [wide_send.at[part] for part in range(HALVES - 1)] + [grad_send.at[0]]:
         all_of(attended_grad_t.at[part_rows(0), 0:three_local], sem)
-    for k in hops:
-        scale_copy(k).wait_send()
-    for copy in gather_copies + full_copies + seq_copies:
-        copy.wait_send()
+    all_of(scale_in.at[0:3], scale_send.at[0])
+    sent(gather_copies)
+    all_of(full.at[0:3], gather_send.at[3])
+    all_of(seq_parts, reduce_send.at[3])
 
     outs = []
     for t, (raw, back, own, out, out_hbm, scale_row, gain_row) in enumerate(
@@ -684,8 +677,7 @@
     for t in range(3):
         count = three_rows if t == 1 else three_parts
         all_of(key_grad_h.at[0:count, :], back_send.at[t])
-    for copy in reduce_copies:
-        copy.wait_send()
+    sent(reduce_copies)
     value_own.wait()
     all_of(value_grad_h.at[0:three_rows, :], value_send.at[0])
     all_of(value_grad_hbm.at[:, 0:three_local], value_recv.at[0])
@@ -700,7 +692,6 @@
     heads = local // HEAD_DIM
     tokens = rows * N_SEQ
     n_z, n_y, n_x = layout
-    dp_count = n_z + n_y + n_x - 3
     token = VMEM((rows, width), BF16)
     by_head = VMEM((heads, tokens, HEAD_DIM), BF16)
     wide = VMEM((tokens, local), BF16)
@@ -779,8 +770,8 @@
             DMA((1,)),
             DMA((4,)),
             DMA((4, heads)),
-            DMA((hops,)),
-            DMA((hops,)),
+            DMA((1,)),
+            DMA((1,)),
             DMA((HALVES,)),
             DMA((HALVES,)),
             DMA((1,)),
@@ -791,10 +782,10 @@
             DMA((3,)),
             DMA((1,)),
             DMA((1,)),
-            DMA((dp_count + hops,)),
-            DMA((dp_count + hops,)),
-            DMA((dp_count + hops,)),
-            DMA((dp_count + hops,)),
+            DMA((4,)),
+            DMA((4,)),
+            DMA((4,)),
+            DMA((4,)),
             DMA((3,)),
             DMA((1,)),
         ],

time: 101 us -> 101 us (level)
  no operation moved by 1% of the time
where the time goes in v7:
time: 101 us; the launch traced here: 100 us
  Pallas kernels  99.8 us (99%)
    pallas_call x1, Pallas kernels, whole_block(): pl.pallas_call(functools.partial(kernel, layout), out_shape=(big, big, bi...  97.2 us
    pallas_call x1, Pallas kernels, results(): pl.pallas_call(functools.partial(results_kernel, factor), out_shape=(*big...  2.54 us

profile of v7, /device:TPU:1, one launch (start us, length us, event | category | flops | bytes accessed | tf_op | source)
XLA Modules:
  0.0 100.4 jit_solution(5820528247345224075)
XLA Ops:
  0.6 97.2 %shard_map.128 = (bf16[192,2560]{1,0:T(8,128)(2,1)S(1)}, bf16[192,2560]{1,0:T(8,128)(2,1)S(1)}, bf16[192,2560]{1,0:T(8,128)(2,1)S(1)}, bf16[192,2560]{1,0:T(8,128)(2,1)S(1)}, f32[8,128]{1,0:T(8,128)S(1)}) custom-call(f32[2,10]{1,0:T(2,128)} %modulation_hbm.1, f32[2,10]{1,0:T(2,128)} %gains_hbm.1, f32[2,2560]{1,0:T(2,128)} %bitcast.1, ...), custom_call_target="tpu_custom_call" | custom-call | tf_op jit(solution)/shard_map/pallas_call | solution.py:707
  97.9 2.5 %shard_map.129 = (bf16[192,2560]{1,0:T(8,128)(2,1)}, bf16[192,2560]{1,0:T(8,128)(2,1)}, bf16[192,2560]{1,0:T(8,128)(2,1)}, bf16[192,2560]{1,0:T(8,128)(2,1)}, f32[5,10]{1,0:T(8,128)}) custom-call(bf16[192,2560]{1,0:T(8,128)(2,1)S(1)} %get-tuple-element.10.refs_0_, bf16[192,2560]{1,0:T(8,128)(2,1)S(1)} %get-tuple-element.11.refs_1_, ...), custom_call_target="tpu_custom_call" | custom-call | tf_op jit(solution)/shard_map/pallas_call | solution.py:816
